TPU v7x, 32 devices: a whole 2x2x4 slice. The times are simulated.
32 devices in a mesh: wide: 8 (over z, y), blk: 4 (over x, core).
Axes of the slice: x: 2, y: 2, z: 4, core: 2. Of those that a mesh axis runs over, the one named last changes fastest.
Arguments:
- embeddings: bfloat16 [4096, 768], P(('wide', 'blk')), may hold values from -100 to 100
- bucket_ids: int32 [4096], P(('wide', 'blk')), may hold values from 0 to 7, as said below
- slot_ids: int32 [4096], P(('wide', 'blk')), may hold values from 0 to 31, as said below
- valid_rows: int32 [4096], P(('wide', 'blk')), may hold values 0 or 1
Outputs:
- neighbour_mean: bfloat16 [4096, 768], P(('wide', 'blk'))
- max_cosine: bfloat16 [4096], P(('wide', 'blk'))
Inputs may be any that keep to these rules, and one draw needn't show every extreme that they name: `bucket_ids`: bucket of each row. Every bucket holds at most 32 rows of one device; some bucket holds exactly 32 rows of every device. `slot_ids`: no two rows of one device share both bucket and slot.
All inputs are finite; a program needn't handle non-finite values. No bound on the sum of `valid_rows` on one device may be relied on, other than what follows from the above.
Results may differ from a plain program's by a relative error of at most 0.003.
Values may be sent and summed in bfloat16 or wider, within the bound.
A program may use at most 64 MiB of HBM per device.

v0:
```python
import functools

import jax
import jax.numpy as jnp
from jax import lax
from jax.experimental import pallas as pl
from jax.experimental.pallas import tpu as pltpu
from jax.sharding import PartitionSpec as P

sharpness = 10.0


def from_behind(value, axis, steps):
    count = lax.axis_size(axis)
    pairs = [(source, (source + steps) % count) for source in range(count)]
    return lax.ppermute(value, axis, pairs)


def unit_rows(embeddings):
    float_rows = embeddings.astype(jnp.float32)
    inverse_norm = lax.rsqrt(jnp.mean(float_rows * float_rows, axis=1, keepdims=True) + 1e-06)
    return (float_rows * inverse_norm).astype(jnp.bfloat16)


def bucket_stats(queries, query_pos, key_rows, key_flags, key_pos):
    feature_count = queries.shape[1]
    cosine = (
        lax.dot_general(
            queries, key_rows, (((1,), (1,)), ((), ())), preferred_element_type=jnp.float32
        )
        / feature_count
    )
    usable = (key_flags[None, :] > 0) & (query_pos[:, None] != key_pos[None, :])
    best_cos = jnp.max(jnp.where(usable, cosine, -1.0), axis=1)
    weights = jnp.where(usable, jnp.exp(sharpness * (cosine - 1.0)), 0.0)
    weight_total = jnp.sum(weights, axis=1)
    summed = jnp.dot(weights.astype(jnp.bfloat16), key_rows, preferred_element_type=jnp.float32)
    return (best_cos, weight_total, summed)


def by_bucket(embeddings, bucket_ids, slot_ids, valid_rows):
    unit_vectors = unit_rows(embeddings)
    row_count, feature_count = unit_vectors.shape
    groups = lax.axis_size("wide")
    blocks = lax.axis_size("blk")
    slot_count = 2 * row_count // groups
    block_rows = groups * slot_count
    cell_ids = bucket_ids * slot_count + slot_ids
    outgoing = jnp.zeros((block_rows, feature_count), jnp.bfloat16).at[cell_ids].set(unit_vectors)
    flag_rows = (
        jnp.zeros((block_rows,), jnp.bfloat16).at[cell_ids].set(valid_rows.astype(jnp.bfloat16))
    )
    arrived, arrived_flags = (
        lax.all_to_all(
            outgoing.reshape(groups, slot_count, feature_count),
            "wide",
            split_axis=0,
            concat_axis=0,
            tiled=True,
        ),
        lax.all_to_all(
            flag_rows.reshape(groups, slot_count), "wide", split_axis=0, concat_axis=0, tiled=True
        ),
    )
    queries = arrived.reshape(block_rows, feature_count)
    query_flags = arrived_flags.reshape(block_rows)
    my_block = lax.axis_index("blk")
    query_pos = my_block * block_rows + jnp.arange(block_rows, dtype=jnp.int32)

    def absorb(running, key_rows, key_flags, key_start):
        key_pos = key_start + jnp.arange(key_rows.shape[0], dtype=jnp.int32)
        best_cos, weight_total, summed = bucket_stats(
            queries, query_pos, key_rows, key_flags, key_pos
        )
        return (jnp.maximum(running[0], best_cos), running[1] + weight_total, running[2] + summed)

    initial = (
        jnp.full((block_rows,), -1.0, jnp.float32),
        jnp.zeros((block_rows,), jnp.float32),
        jnp.zeros((block_rows, feature_count), jnp.float32),
    )
    key_rows, key_flags = (queries, query_flags)
    running = absorb(initial, key_rows, key_flags, my_block * block_rows)
    for turn_index in range(1, blocks):
        key_rows, key_flags = from_behind((key_rows, key_flags), "blk", 1)
        running = absorb(
            running, key_rows, key_flags, (my_block - turn_index) % blocks * block_rows
        )
    best_cos, weight_total, summed = running
    mean_rows = ((queries.astype(jnp.float32) + summed) / (1.0 + weight_total[:, None])).astype(
        jnp.bfloat16
    )
    back_mean, back_best = (
        lax.all_to_all(
            mean_rows.reshape(groups, slot_count, feature_count),
            "wide",
            split_axis=0,
            concat_axis=0,
            tiled=True,
        ),
        lax.all_to_all(
            best_cos.astype(jnp.bfloat16).reshape(groups, slot_count),
            "wide",
            split_axis=0,
            concat_axis=0,
            tiled=True,
        ),
    )
    neighbour_mean = back_mean.reshape(block_rows, feature_count)[cell_ids]
    max_cosine = back_best.reshape(block_rows)[cell_ids]
    return (neighbour_mean, max_cosine)


PAIR = 2
PIECES = 4
GRANT = 56_240_000


def arrival_order(place, count):
    low, high = place, count - 1 - place
    order = []
    for distance in range(1, count):
        if distance <= low:
            order.append(place - distance)
        if distance <= high:
            order.append(place + distance)
    if low == 0 or high == 0:
        order = [order[1], order[1]] + order[2:]
    return order


def dense_kernel(
    planes, emb_hbm, bucket_hbm, valid_hbm, mean_ref, best_ref,
    emb_ref, bucket_ref, valid_ref, load_sem,
    keys, key_meta, queries, query_meta, query_col, total, peak, weight,
    part_out, part_in, stat_out, stat_in,
    plane_keys, plane_meta, help_total, help_peak, help_weight,
    help_out, help_in, help_stat_out, help_stat_in,
    z_send, z_recv, zm_send, zm_recv, c_send, c_recv, cm_send, cm_recv,
    q_send, q_recv, qm_send, qm_recv, p_send, p_recv, s_send, s_recv,
    f_send, f_recv, fm_send, fm_recv, h_send, h_recv,
):
    rows, features = emb_ref.shape
    spots = queries.shape[0]
    wide, blk = lax.axis_index("wide"), lax.axis_index("blk")
    z, y = lax.div(wide, PAIR), lax.rem(wide, PAIR)
    x, core = lax.div(blk, PAIR), lax.rem(blk, PAIR)
    other = 1 - core
    columns = spots // PAIR
    piece = rows // PIECES

    def at(z_at, y_at, x_at, core_at):
        return (z_at * PAIR + y_at, x_at * PAIR + core_at)

    def spot_device(spot):
        dy, dx = divmod(spot, columns)
        return at(z, lax.rem(y + dy, PAIR), lax.rem(x + dx, columns), core)

    def seen_from(spot):
        dy, dx = divmod(spot, columns)
        return (-dy) % PAIR * columns + (-dx) % columns

    def remote(source, target, send, recv, device):
        return pltpu.make_async_remote_copy(
            src_ref=source, dst_ref=target, send_sem=send, recv_sem=recv,
            device_id=device, device_id_type=pl.DeviceIdType.MESH,
        )

    partner = at(z, y, x, other)
    has_low, has_high = z > 0, z < planes - 1

    loads = [
        pltpu.make_async_copy(source, target, load_sem.at[index])
        for index, (source, target) in enumerate(
            ((emb_hbm, emb_ref), (bucket_hbm, bucket_ref), (valid_hbm, valid_ref))
        )
    ]
    for load in loads:
        load.start()

    barrier = pltpu.get_barrier_semaphore()

    def greet(device):
        pl.semaphore_signal(barrier, inc=1, device_id=device, device_id_type=pl.DeviceIdType.MESH)

    greet(partner)
    for spot in range(1, spots):
        greet(spot_device(spot))

    @pl.when(has_low)
    def _():
        greet(at(z - 1, y, x, core))

    @pl.when(has_high)
    def _():
        greet(at(z + 1, y, x, core))

    for load in loads:
        load.wait()
    floats = emb_ref[...].astype(jnp.float32)
    inverse = lax.rsqrt(jnp.mean(floats * floats, axis=1, keepdims=True) + 1e-06)
    unit = (floats * inverse).astype(jnp.bfloat16)
    keys[z, core] = unit
    queries[0] = unit
    meta = jnp.concatenate([bucket_ref[...], valid_ref[...]], axis=0).astype(jnp.float32)
    key_meta[z, core] = meta
    query_meta[0] = meta

    pl.semaphore_wait(barrier, jnp.where(has_low & has_high, spots + 2, spots + 1))

    def z_meta(source, way, to):
        ref = key_meta.at[source, core]
        return remote(
            ref, ref, zm_send.at[source, way], zm_recv.at[source], at(to, y, x, core)
        )

    def z_copy(source, way, to, part):
        ref = keys.at[source, core, pl.ds(part * piece, piece)]
        return remote(
            ref, ref, z_send.at[source, way, part], z_recv.at[source, part], at(to, y, x, core)
        )

    def c_meta(source, side):
        ref = key_meta.at[source, side]
        return remote(ref, ref, cm_send.at[source], cm_recv.at[source], partner)

    def c_copy(source, side, part):
        ref = keys.at[source, side, pl.ds(part * piece, piece)]
        return remote(ref, ref, c_send.at[source, part], c_recv.at[source, part], partner)

    def q_meta(spot):
        mine = seen_from(spot)
        return remote(
            query_meta.at[0], query_meta.at[mine], qm_send.at[spot], qm_recv.at[mine],
            spot_device(spot),
        )

    def q_copy(spot):
        mine = seen_from(spot)
        return remote(
            queries.at[0], queries.at[mine], q_send.at[spot], q_recv.at[mine], spot_device(spot)
        )

    def send_ways(source, act):
        @pl.when(has_high & ((source < z) | ((source == z) & (z < planes - 2))))
        def _():
            act(1, z + 1)

        @pl.when(has_low & ((source > z) | ((source == z) & (z > 1))))
        def _():
            act(0, z - 1)

    send_ways(z, lambda way, to: z_meta(z, way, to).start())
    for part in range(PIECES):
        send_ways(z, lambda way, to: z_copy(z, way, to, part).start())
    c_meta(z, core).start()
    for part in range(PIECES):
        c_copy(z, core, part).start()
    for spot in range(spots - 1, 0, -1):
        q_meta(spot).start()
        q_copy(spot).start()

    def column_of(spot):
        row = query_meta[spot, 0:1, :]
        query_col[spot] = jnp.transpose(jnp.broadcast_to(row, (rows, rows)))

    def terms(chosen, buckets, block, metas, own_keys):
        count = chosen.shape[0]
        cosine = lax.dot_general(
            chosen, block, (((1,), (1,)), ((), ())), preferred_element_type=jnp.float32
        ) * (1.0 / features)
        line = lax.broadcasted_iota(jnp.int32, (count, rows), 0)
        lane = lax.broadcasted_iota(jnp.int32, (count, rows), 1)
        factors = []
        peaks = None
        sums = None
        for index, (meta, own) in enumerate(zip(metas, own_keys)):
            wanted = jnp.where(meta[1:2, :] > 0, meta[0:1, :], -1.0)
            usable = buckets == wanted
            if own is not None:
                shift = jnp.where(own, 0, count + rows)
                usable = usable & (line + shift != lane)
            values = cosine[:, index * rows : (index + 1) * rows]
            best = jnp.where(usable, values, -1.0)
            factor = jnp.where(usable, jnp.exp(sharpness * (values - 1.0)), 0.0)
            factors.append(factor.astype(jnp.bfloat16))
            peaks = best if peaks is None else jnp.maximum(peaks, best)
            sums = factor if sums is None else sums + factor
        summed = jnp.dot(
            jnp.concatenate(factors, axis=1), block, preferred_element_type=jnp.float32
        )
        return peaks, sums, summed

    def absorb(first, last, source, fresh, sides=tuple(range(PAIR))):
        count = (last - first) * rows
        if len(sides) == PAIR:
            block = keys[source].reshape(PAIR * rows, features)
        else:
            block = keys[source, sides[0]]
        peaks, sums, summed = terms(
            queries[first:last].reshape(count, features),
            query_col[first:last].reshape(count, rows),
            block,
            [key_meta[source, side] for side in sides],
            [(source == z) & (core == side) if first == 0 else None for side in sides],
        )
        part = (last - first, rows)
        if fresh:
            peak[first:last] = peaks.reshape(*part, rows)
            weight[first:last] = sums.reshape(*part, rows)
            total[first:last] = summed.reshape(*part, features)
        else:
            peak[first:last] = jnp.maximum(peak[first:last], peaks.reshape(*part, rows))
            weight[first:last] += sums.reshape(*part, rows)
            total[first:last] += summed.reshape(*part, features)

    def wait_partner(source):
        c_meta(source, other).wait_recv()
        for part in range(PIECES):
            c_copy(source, other, part).wait_recv()

    def take(*arriving):
        for source in arriving:
            z_meta(source, 0, z).wait_recv()
            send_ways(source, lambda way, to: z_meta(source, way, to).start())
            c_meta(source, core).start()
        for part in range(PIECES):
            for source in arriving:
                z_copy(source, 0, z, part).wait_recv()
                send_ways(source, lambda way, to: z_copy(source, way, to, part).start())
                c_copy(source, core, part).start()

    orders = [arrival_order(place, planes) for place in range(planes)]

    def source_at(turn):
        source = jnp.int32(orders[0][turn])
        for place in range(1, planes):
            source = jnp.where(z == place, orders[place][turn], source)
        return source

    sources = [source_at(turn) for turn in range(planes - 1)]
    inner = has_low & has_high
    final = sources[-1]

    def at_end(source):
        @pl.when(jnp.logical_not(inner))
        def _():
            take(source)

    column_of(0)
    wait_partner(z)
    absorb(0, 1, z, True)

    @pl.when(inner)
    def _():
        take(*sources[:2])
        for source in sources[2:]:
            take(source)

    def each_source(act):
        for turn, source in enumerate(sources[:-1]):
            if turn == 1:

                @pl.when(inner)
                def _():
                    act(source)
            else:
                act(source)

    at_end(sources[0])
    for source in sources[2:-1]:
        at_end(source)

    def own_rows(source):
        wait_partner(source)
        absorb(0, 1, source, False)

    each_source(own_rows)

    def f_copies(spot):
        return (
            remote(
                query_meta.at[spot], plane_meta.at[spot], fm_send.at[spot], fm_recv.at[spot], partner
            ),
            remote(queries.at[spot], plane_keys.at[spot], f_send.at[spot], f_recv.at[spot], partner),
        )

    helper = (z == 1) | (z == planes - 2)
    end_z = jnp.where(z == 1, 0, planes - 1)

    for spot in range(1, spots):
        q_meta(seen_from(spot)).wait_recv()
        column_of(spot)
        q_copy(seen_from(spot)).wait_recv()

        @pl.when(helper)
        def _():
            for copy in f_copies(spot):
                copy.start()

    def h_copies():
        device = at(jnp.where(helper, end_z, z), y, x, core)
        return (
            remote(help_stat_out, help_stat_in, h_send.at[0], h_recv.at[0], device),
            remote(help_out, help_in, h_send.at[1], h_recv.at[1], device),
        )

    absorb(1, spots, z, True)

    each_source(lambda source: absorb(1, spots, source, False))
    at_end(final)
    absorb(1, spots, final, False, (core,))
    wait_partner(final)

    def stat_rows(spot):
        top = jnp.max(jnp.transpose(peak[spot]), axis=0, keepdims=True)
        mass = jnp.sum(jnp.transpose(weight[spot]), axis=0, keepdims=True)
        return top, mass

    across, along = columns, 1
    corner = across + along
    half = rows // 2
    halves = (pl.ds(0, half), pl.ds(half, half))

    def p_copy(spot, side):
        mine = seen_from(spot)
        return remote(
            part_out.at[spot, halves[side]], part_in.at[mine, halves[side]],
            p_send.at[spot, side], p_recv.at[mine, side], spot_device(spot),
        )

    def corner_copy(side):
        spot = (along, across)[side]
        return remote(
            part_out.at[corner, halves[side]], part_in.at[corner, halves[side]],
            p_send.at[corner, side], p_recv.at[corner, side], spot_device(spot),
        )

    def s_copy(spot):
        mine = seen_from(spot)
        return remote(
            stat_out.at[spot], stat_in.at[mine], s_send.at[spot], s_recv.at[mine],
            spot_device(spot),
        )

    absorb(corner, corner + 1, final, False, (other,))
    part_out[corner] = total[corner].astype(jnp.bfloat16)
    corner_copy(0).start()
    corner_copy(1).start()
    passing = ((along, 1), (across, 0))
    for spot, side in passing:
        absorb(spot, spot + 1, final, False, (other,))
        part_out[spot, halves[1 - side]] = total[spot, halves[1 - side]].astype(jnp.bfloat16)
        p_copy(spot, 1 - side).start()
    for spot in range(spots - 1, 0, -1):
        stat_out[spot] = jnp.concatenate(stat_rows(spot), axis=0)
        s_copy(spot).start()
    @pl.when(helper)
    def _():
        row = key_meta[end_z, core, 0:1, :]
        column = jnp.transpose(jnp.broadcast_to(row, (rows, rows)))
        for spot in range(spots):
            if spot == 0:
                second, second_meta = keys[z, other], key_meta[z, other]
            else:
                for copy in f_copies(spot):
                    copy.wait_recv()
                second, second_meta = plane_keys[spot], plane_meta[spot]
            peaks, sums, summed = terms(
                keys[end_z, core],
                column,
                jnp.concatenate([queries[spot], second], axis=0),
                [query_meta[spot], second_meta],
                [None, None],
            )
            if spot == 0:
                help_peak[...] = peaks
                help_weight[...] = sums
                help_total[...] = summed
            else:
                help_peak[...] = jnp.maximum(help_peak[...], peaks)
                help_weight[...] += sums
                help_total[...] += summed
        help_out[...] = help_total[...].astype(jnp.bfloat16)
        top = jnp.max(jnp.transpose(help_peak[...]), axis=0, keepdims=True)
        mass = jnp.sum(jnp.transpose(help_weight[...]), axis=0, keepdims=True)
        help_stat_out[...] = jnp.concatenate([top, mass], axis=0)
        for copy in h_copies():
            copy.start()

    for spot, side in passing:
        corner_copy(side).wait_recv()
        part_out[spot, halves[side]] = (
            total[spot, halves[side]] + part_in[corner, halves[side]].astype(jnp.float32)
        ).astype(jnp.bfloat16)
        p_copy(spot, side).start()

    absorb(0, 1, final, False)
    stat_in[0] = jnp.concatenate(stat_rows(0), axis=0)
    total[0] += queries[0].astype(jnp.float32)

    @pl.when(jnp.logical_not(inner))
    def _():
        for copy in h_copies():
            copy.wait_recv()
        stat_in[0] = jnp.concatenate(
            [
                jnp.maximum(stat_in[0, 0:1, :], help_stat_in[0:1, :]),
                stat_in[0, 1:2, :] + help_stat_in[1:2, :],
            ],
            axis=0,
        )
        total[0] += help_in[...].astype(jnp.float32)

    top, mass = stat_in[0, 0:1, :], stat_in[0, 1:2, :]
    for spot in range(1, spots):
        s_copy(seen_from(spot)).wait_recv()
        top = jnp.maximum(top, stat_in[spot, 0:1, :])
        mass = mass + stat_in[spot, 1:2, :]
    best_ref[...] = top.astype(jnp.bfloat16)
    below = jnp.transpose(jnp.broadcast_to(1.0 + mass, (rows, rows)))[:, 0:1]
    for spot, _ in passing:
        for side in range(2):
            p_copy(seen_from(spot), side).wait_recv()
    result = total[0]
    for spot, _ in passing:
        result = result + part_in[spot].astype(jnp.float32)
    mean_ref[...] = (result / below).astype(jnp.bfloat16)

    send_ways(z, lambda way, to: z_meta(z, way, to).wait_send())
    for part in range(PIECES):
        send_ways(z, lambda way, to: z_copy(z, way, to, part).wait_send())
    c_meta(z, core).wait_send()
    for part in range(PIECES):
        c_copy(z, core, part).wait_send()
    def sent(source):
        send_ways(source, lambda way, to: z_meta(source, way, to).wait_send())
        c_meta(source, core).wait_send()
        for part in range(PIECES):
            send_ways(source, lambda way, to: z_copy(source, way, to, part).wait_send())
            c_copy(source, core, part).wait_send()

    each_source(sent)
    sent(final)

    @pl.when(helper)
    def _():
        for spot in range(1, spots):
            for copy in f_copies(spot):
                copy.wait_send()
        for copy in h_copies():
            copy.wait_send()

    for spot in range(1, spots):
        q_meta(spot).wait_send()
        q_copy(spot).wait_send()
        s_copy(spot).wait_send()
    for side in range(2):
        corner_copy(side).wait_send()
        for spot, _ in passing:
            p_copy(spot, side).wait_send()


def dense(embeddings, bucket_ids, valid_rows):
    rows, features = embeddings.shape
    planes = lax.axis_size("wide") // PAIR
    spots = lax.axis_size("blk")
    dma = pltpu.SemaphoreType.DMA
    vmem = pl.BlockSpec(memory_space=pltpu.VMEM)
    mean, best = pl.pallas_call(
        functools.partial(dense_kernel, planes),
        out_shape=(
            jax.ShapeDtypeStruct((rows, features), jnp.bfloat16),
            jax.ShapeDtypeStruct((1, rows), jnp.bfloat16),
        ),
        in_specs=[pl.BlockSpec(memory_space=pltpu.HBM)] * 3,
        out_specs=(vmem, vmem),
        scratch_shapes=[
            pltpu.VMEM((rows, features), jnp.bfloat16),
            pltpu.VMEM((1, rows), jnp.int32),
            pltpu.VMEM((1, rows), jnp.int32),
            dma((3,)),
            pltpu.VMEM((planes, PAIR, rows, features), jnp.bfloat16),
            pltpu.VMEM((planes, PAIR, 2, rows), jnp.float32),
            pltpu.VMEM((spots, rows, features), jnp.bfloat16),
            pltpu.VMEM((spots, 2, rows), jnp.float32),
            pltpu.VMEM((spots, rows, rows), jnp.float32),
            pltpu.VMEM((spots, rows, features), jnp.float32),
            pltpu.VMEM((spots, rows, rows), jnp.float32),
            pltpu.VMEM((spots, rows, rows), jnp.float32),
            pltpu.VMEM((spots, rows, features), jnp.bfloat16),
            pltpu.VMEM((spots, rows, features), jnp.bfloat16),
            pltpu.VMEM((spots, 2, rows), jnp.float32),
            pltpu.VMEM((spots, 2, rows), jnp.float32),
            pltpu.VMEM((spots, rows, features), jnp.bfloat16),
            pltpu.VMEM((spots, 2, rows), jnp.float32),
            pltpu.VMEM((rows, features), jnp.float32),
            pltpu.VMEM((rows, rows), jnp.float32),
            pltpu.VMEM((rows, rows), jnp.float32),
            pltpu.VMEM((rows, features), jnp.bfloat16),
            pltpu.VMEM((rows, features), jnp.bfloat16),
            pltpu.VMEM((2, rows), jnp.float32),
            pltpu.VMEM((2, rows), jnp.float32),
            dma((planes, 2, PIECES)), dma((planes, PIECES)), dma((planes, 2)), dma((planes,)),
            dma((planes, PIECES)), dma((planes, PIECES)), dma((planes,)), dma((planes,)),
            dma((spots,)), dma((spots,)), dma((spots,)), dma((spots,)),
            dma((spots, 2)), dma((spots, 2)), dma((spots,)), dma((spots,)),
            dma((spots,)), dma((spots,)), dma((spots,)), dma((spots,)), dma((2,)), dma((2,)),
        ],
        compiler_params=pltpu.CompilerParams(
            collective_id=0, has_side_effects=True, vmem_limit_bytes=GRANT
        ),
    )(embeddings, bucket_ids.reshape(1, rows), valid_rows.reshape(1, rows))
    return mean, best.reshape(rows)


def on_device(embeddings, bucket_ids, slot_ids, valid_rows):
    rows = embeddings.shape[0]
    groups = lax.axis_size("wide")
    blocks = lax.axis_size("blk")
    bucket_work = blocks * (2 * rows) ** 2
    dense_work = groups * blocks * rows**2
    fits = groups % PAIR == 0 and groups >= 4 * PAIR and blocks == PAIR * PAIR and rows == 128
    if fits and dense_work <= 4 * bucket_work:
        return dense(embeddings, bucket_ids, valid_rows)
    return by_bucket(embeddings, bucket_ids, slot_ids, valid_rows)


def solution(mesh):
    in_specs = (
        P(("wide", "blk"), None),
        P(("wide", "blk")),
        P(("wide", "blk")),
        P(("wide", "blk")),
    )
    out_specs = (P(("wide", "blk"), None), P(("wide", "blk")))
    return jax.shard_map(
        on_device, mesh=mesh, in_specs=in_specs, out_specs=out_specs, check_vma=False
    )
```

profile of v0, /device:TPU:0, one launch (start us, length us, event | category | flops | bytes accessed | tf_op | source)
XLA Modules:
  0.0 32.4 jit_solution(17758499344465518930)
XLA Ops:
  0.6 0.0 copy-start
  0.6 0.0 copy-start.1
  0.6 0.6 %copy-done = s32[128]{0:T(128)S(1)} copy-done((s32[128]{0:T(128)S(1)}, s32[128]{0:T(128)}, u32[]{:S(2)}) %copy-start) | copy-done | bytes 536
  1.3 0.0 copy-done.1
  1.3 29.9 %shard_map.50 = (bf16[128,768]{1,0:T(8,128)(2,1)S(1)}, bf16[1,128]{1,0:T(2,128)(2,1)S(1)}) custom-call(bf16[128,768]{1,0:T(8,128)(2,1)} %emb_hbm.1, s32[1,128]{1,0:T(1,128)S(1)} %bitcast.3, s32[1,128]{1,0:T(1,128)S(1)} %bitcast.4), custom_call_target="tpu_custom_call" | custom-call | tf_op jit(solution)/shard_map/pallas_call | solution.py:570
  31.3 0.7 %copy.7 = bf16[128,768]{1,0:T(8,128)(2,1)} copy(bf16[128,768]{1,0:T(8,128)(2,1)S(1)} %get-tuple-element.8) | data formatting | bytes 393216
  31.9 0.5 %copy.8 = bf16[128]{0:T(256)(128)(2,1)} copy(bf16[128]{0:T(256)(128)(2,1)S(1)} %bitcast.5) | data formatting | bytes 512
Async XLA Ops:
  0.6 0.7 %copy-start = (s32[128]{0:T(128)S(1)}, s32[128]{0:T(128)}, u32[]{:S(2)}) copy-start(s32[128]{0:T(128)} %param.5) | copy-start | bytes 1540
  0.6 0.7 %copy-start.1 = (s32[128]{0:T(128)S(1)}, s32[128]{0:T(128)}, u32[]{:S(2)}) copy-start(s32[128]{0:T(128)} %param.6) | copy-start | bytes 1540
where the time goes:
time: 32.6 us; the launch traced here: 32.4 us
  Pallas kernels  29.9 us (92%)
  local copies, waits for them, and re-layouts  1.85 us (6%)
  between operations  0.66 us (2%)
    pallas_call x1, Pallas kernels, dense(): pl.pallas_call(functools.partial(dense_kernel, planes), out_shape=(jax.Sh...  29.9 us
    unnamed x6, local copies, waits for them, and re-layouts  1.85 us

commit v1 on v0

--- a/solution.py
+++ b/solution.py
@@ -517,7 +517,7 @@
         s_copy(seen_from(spot)).wait_recv()
         top = jnp.maximum(top, stat_in[spot, 0:1, :])
         mass = mass + stat_in[spot, 1:2, :]
-    best_ref[...] = top.astype(jnp.bfloat16)
+    best_ref[...] = top
     below = jnp.transpose(jnp.broadcast_to(1.0 + mass, (rows, rows)))[:, 0:1]
     for spot, _ in passing:
         for side in range(2):
@@ -561,6 +561,35 @@
             p_copy(spot, side).wait_send()
 
 
+def finish_kernel(mean_ref, best_ref, mean_out, best_out, line, sem):
+    line[...] = best_ref[0].astype(jnp.bfloat16)
+    copies = [
+        pltpu.make_async_copy(mean_ref, mean_out, sem.at[0]),
+        pltpu.make_async_copy(line, best_out, sem.at[1]),
+    ]
+    for copy in copies:
+        copy.start()
+    for copy in copies:
+        copy.wait()
+
+
+def finish(mean, best):
+    rows, features = mean.shape
+    vmem = pl.BlockSpec(memory_space=pltpu.VMEM)
+    hbm = pl.BlockSpec(memory_space=pltpu.HBM)
+    return pl.pallas_call(
+        finish_kernel,
+        out_shape=(
+            jax.ShapeDtypeStruct((rows, features), jnp.bfloat16),
+            jax.ShapeDtypeStruct((rows,), jnp.bfloat16),
+        ),
+        in_specs=[vmem, vmem],
+        out_specs=(hbm, hbm),
+        scratch_shapes=[pltpu.VMEM((rows,), jnp.bfloat16), pltpu.SemaphoreType.DMA((2,))],
+        compiler_params=pltpu.CompilerParams(vmem_limit_bytes=4_000_000),
+    )(mean, best)
+
+
 def dense(embeddings, bucket_ids, valid_rows):
     rows, features = embeddings.shape
     planes = lax.axis_size("wide") // PAIR
@@ -571,7 +600,7 @@
         functools.partial(dense_kernel, planes),
         out_shape=(
             jax.ShapeDtypeStruct((rows, features), jnp.bfloat16),
-            jax.ShapeDtypeStruct((1, rows), jnp.bfloat16),
+            jax.ShapeDtypeStruct((1, rows), jnp.float32),
         ),
         in_specs=[pl.BlockSpec(memory_space=pltpu.HBM)] * 3,
         out_specs=(vmem, vmem),
@@ -610,8 +639,8 @@
         compiler_params=pltpu.CompilerParams(
             collective_id=0, has_side_effects=True, vmem_limit_bytes=GRANT
         ),
-    )(embeddings, bucket_ids.reshape(1, rows), valid_rows.reshape(1, rows))
-    return mean, best.reshape(rows)
+    )(*[pltpu.with_memory_space_constraint(v, pltpu.HBM) for v in (embeddings, bucket_ids.reshape(1, rows), valid_rows.reshape(1, rows))])
+    return finish(mean, best)
 
 
 def on_device(embeddings, bucket_ids, slot_ids, valid_rows):

time: 32.6 us -> 31.5 us (0.966)
  local copies, waits for them, and re-layouts: 1.85 us -> 0 us
  Pallas kernels: 29.9 us -> 30.7 us
    unnamed x6 -> x0, local copies, waits for them, and re-layouts: 1.85 us -> none
    pallas_call x0 -> x1, Pallas kernels: none -> 0.7 us  [finish(): pl.pallas_call(finish_kernel, out_shape=(jax.ShapeDtypeStruct((rows, feat...]
where the time goes in v1:
time: 31.5 us; the launch traced here: 31.3 us
  Pallas kernels  30.7 us (97%)
  between operations  0.64 us (2%)
    pallas_call x1, Pallas kernels, dense(): pl.pallas_call(functools.partial(dense_kernel, planes), out_shape=(jax.Sh...  30 us
    pallas_call x1, Pallas kernels, finish(): pl.pallas_call(finish_kernel, out_shape=(jax.ShapeDtypeStruct((rows, feat...  0.7 us

profile of v1, /device:TPU:0, one launch (start us, length us, event | category | flops | bytes accessed | tf_op | source)
XLA Modules:
  0.0 31.3 jit_solution(12162142187371386462)
XLA Ops:
  0.6 30.0 %shard_map.50 = (bf16[128,768]{1,0:T(8,128)(2,1)S(1)}, f32[1,128]{1,0:T(1,128)S(1)}) custom-call(bf16[128,768]{1,0:T(8,128)(2,1)} %emb_hbm.1, s32[1,128]{1,0:T(1,128)} %bitcast.2, s32[1,128]{1,0:T(1,128)} %bitcast.3), custom_call_target="tpu_custom_call" | custom-call | tf_op jit(solution)/shard_map/pallas_call | solution.py:599
  30.6 0.7 %shard_map.51 = (bf16[128,768]{1,0:T(8,128)(2,1)}, bf16[128]{0:T(256)(128)(2,1)}) custom-call(bf16[128,768]{1,0:T(8,128)(2,1)S(1)} %get-tuple-element.4.mean_ref, f32[1,128]{1,0:T(1,128)S(1)} %get-tuple-element.5.best_ref), custom_call_target="tpu_custom_call" | custom-call | tf_op jit(solution)/shard_map/pallas_call | solution.py:580

commit v2 on v1

v2 whole, which is shorter than its diff:
```python
import functools

import jax
import jax.numpy as jnp
from jax import lax
from jax.experimental import pallas as pl
from jax.experimental.pallas import tpu as pltpu
from jax.sharding import PartitionSpec as P

sharpness = 10.0


def from_behind(value, axis, steps):
    count = lax.axis_size(axis)
    pairs = [(source, (source + steps) % count) for source in range(count)]
    return lax.ppermute(value, axis, pairs)


def unit_rows(embeddings):
    float_rows = embeddings.astype(jnp.float32)
    inverse_norm = lax.rsqrt(jnp.mean(float_rows * float_rows, axis=1, keepdims=True) + 1e-06)
    return (float_rows * inverse_norm).astype(jnp.bfloat16)


def bucket_stats(queries, query_pos, key_rows, key_flags, key_pos):
    feature_count = queries.shape[1]
    cosine = (
        lax.dot_general(
            queries, key_rows, (((1,), (1,)), ((), ())), preferred_element_type=jnp.float32
        )
        / feature_count
    )
    usable = (key_flags[None, :] > 0) & (query_pos[:, None] != key_pos[None, :])
    best_cos = jnp.max(jnp.where(usable, cosine, -1.0), axis=1)
    weights = jnp.where(usable, jnp.exp(sharpness * (cosine - 1.0)), 0.0)
    weight_total = jnp.sum(weights, axis=1)
    summed = jnp.dot(weights.astype(jnp.bfloat16), key_rows, preferred_element_type=jnp.float32)
    return (best_cos, weight_total, summed)


def by_bucket(embeddings, bucket_ids, slot_ids, valid_rows):
    unit_vectors = unit_rows(embeddings)
    row_count, feature_count = unit_vectors.shape
    groups = lax.axis_size("wide")
    blocks = lax.axis_size("blk")
    slot_count = 2 * row_count // groups
    block_rows = groups * slot_count
    cell_ids = bucket_ids * slot_count + slot_ids
    outgoing = jnp.zeros((block_rows, feature_count), jnp.bfloat16).at[cell_ids].set(unit_vectors)
    flag_rows = (
        jnp.zeros((block_rows,), jnp.bfloat16).at[cell_ids].set(valid_rows.astype(jnp.bfloat16))
    )
    arrived, arrived_flags = (
        lax.all_to_all(
            outgoing.reshape(groups, slot_count, feature_count),
            "wide",
            split_axis=0,
            concat_axis=0,
            tiled=True,
        ),
        lax.all_to_all(
            flag_rows.reshape(groups, slot_count), "wide", split_axis=0, concat_axis=0, tiled=True
        ),
    )
    queries = arrived.reshape(block_rows, feature_count)
    query_flags = arrived_flags.reshape(block_rows)
    my_block = lax.axis_index("blk")
    query_pos = my_block * block_rows + jnp.arange(block_rows, dtype=jnp.int32)

    def absorb(running, key_rows, key_flags, key_start):
        key_pos = key_start + jnp.arange(key_rows.shape[0], dtype=jnp.int32)
        best_cos, weight_total, summed = bucket_stats(
            queries, query_pos, key_rows, key_flags, key_pos
        )
        return (jnp.maximum(running[0], best_cos), running[1] + weight_total, running[2] + summed)

    initial = (
        jnp.full((block_rows,), -1.0, jnp.float32),
        jnp.zeros((block_rows,), jnp.float32),
        jnp.zeros((block_rows, feature_count), jnp.float32),
    )
    key_rows, key_flags = (queries, query_flags)
    running = absorb(initial, key_rows, key_flags, my_block * block_rows)
    for turn_index in range(1, blocks):
        key_rows, key_flags = from_behind((key_rows, key_flags), "blk", 1)
        running = absorb(
            running, key_rows, key_flags, (my_block - turn_index) % blocks * block_rows
        )
    best_cos, weight_total, summed = running
    mean_rows = ((queries.astype(jnp.float32) + summed) / (1.0 + weight_total[:, None])).astype(
        jnp.bfloat16
    )
    back_mean, back_best = (
        lax.all_to_all(
            mean_rows.reshape(groups, slot_count, feature_count),
            "wide",
            split_axis=0,
            concat_axis=0,
            tiled=True,
        ),
        lax.all_to_all(
            best_cos.astype(jnp.bfloat16).reshape(groups, slot_count),
            "wide",
            split_axis=0,
            concat_axis=0,
            tiled=True,
        ),
    )
    neighbour_mean = back_mean.reshape(block_rows, feature_count)[cell_ids]
    max_cosine = back_best.reshape(block_rows)[cell_ids]
    return (neighbour_mean, max_cosine)


PAIR = 2
PLANES = 4
SPOTS = PAIR * PAIR
PIECES = 4
GRANT = 56_240_000


def dense_kernel(
    emb_hbm, bucket_hbm, valid_hbm, mean_ref, best_ref,
    emb_ref, bucket_ref, valid_ref,
    keys, key_meta, plane, spot_meta, plane_meta, query_col, total, peak, weight,
    part_out, part_in, stat_out, stat_in, help_out, help_in, help_stat_out, help_stat_in,
    load_sem, z_send, z_recv, zm_send, zm_recv, c_send, c_recv, cm_send, cm_recv,
    q_send, q_recv, qm_send, qm_recv, f_send, f_recv,
    p_send, corner_recv, p_recv, s_send, sc_recv, s_recv, h_send, h_recv,
):
    rows, features = emb_ref.shape
    piece = rows // PIECES
    half = rows // 2
    halves = (pl.ds(0, half), pl.ds(half, half))
    wide, blk = lax.axis_index("wide"), lax.axis_index("blk")
    z, y = lax.div(wide, PAIR), lax.rem(wide, PAIR)
    x, core = lax.div(blk, PAIR), lax.rem(blk, PAIR)
    beside_x, beside_y, corner = 1, 2, 3

    def at(z_at, y_at, x_at, core_at):
        return (z_at * PAIR + y_at, x_at * PAIR + core_at)

    partner = at(z, y, x, 1 - core)
    x_device = at(z, y, 1 - x, core)
    y_device = at(z, 1 - y, x, core)
    inner = (z > 0) & (z < PLANES - 1)
    lower = z < PLANES // 2
    across_z = PLANES - 1 - z
    end_device = at(jnp.where(lower, 0, PLANES - 1), y, x, core)
    next_device = at(jnp.where(lower, 1, PLANES - 2), y, x, core)
    far_device = at(across_z, y, x, core)

    def remote(source, target, send, recv, device):
        return pltpu.make_async_remote_copy(
            src_ref=source, dst_ref=target, send_sem=send, recv_sem=recv,
            device_id=device, device_id_type=pl.DeviceIdType.MESH,
        )

    def arrived(ref, recv):
        remote(ref, ref, recv, recv, partner).wait_recv()

    def sent(ref, send):
        remote(ref, ref, send, send, partner).wait_send()

    loads = [
        pltpu.make_async_copy(source, target, load_sem.at[index])
        for index, (source, target) in enumerate(
            ((emb_hbm, emb_ref), (bucket_hbm, bucket_ref), (valid_hbm, valid_ref))
        )
    ]
    for load in loads:
        load.start()

    barrier = pltpu.get_barrier_semaphore()

    def greet(device):
        pl.semaphore_signal(barrier, inc=1, device_id=device, device_id_type=pl.DeviceIdType.MESH)

    greet(x_device)
    greet(y_device)
    greet(partner)

    @pl.when(inner)
    def _():
        greet(far_device)
        greet(end_device)

    @pl.when(jnp.logical_not(inner))
    def _():
        greet(next_device)

    for load in loads:
        load.wait()
    floats = emb_ref[...].astype(jnp.float32)
    inverse = lax.rsqrt(jnp.mean(floats * floats, axis=1, keepdims=True) + 1e-06)
    unit = (floats * inverse).astype(jnp.bfloat16)
    own = jnp.where(inner, 1, 0)
    keys[own, 0] = unit
    buckets = bucket_ref[...].astype(jnp.float32)
    meta = jnp.concatenate([buckets, jnp.where(valid_ref[...] > 0, buckets, -1.0)], axis=0)
    key_meta[own, 0] = meta
    spot_meta[0] = meta

    pl.semaphore_wait(barrier, jnp.where(inner, 5, 4))

    def column(row):
        return jnp.transpose(jnp.broadcast_to(row, (rows, rows)))

    def terms(chosen, buckets, block, metas, itself):
        cosine = lax.dot_general(
            chosen, block, (((1,), (1,)), ((), ())), preferred_element_type=jnp.float32
        ) * (1.0 / features)
        factors = []
        peaks = None
        sums = None
        for index, meta in enumerate(metas):
            usable = buckets == meta[1:2, :]
            if index == itself:
                line = lax.broadcasted_iota(jnp.int32, (rows, rows), 0)
                lane = lax.broadcasted_iota(jnp.int32, (rows, rows), 1)
                usable = usable & (line != lane)
            values = cosine[:, index * rows : (index + 1) * rows]
            best = jnp.where(usable, values, -1.0)
            factor = jnp.where(usable, jnp.exp(sharpness * (values - 1.0)), 0.0)
            factors.append(factor.astype(jnp.bfloat16))
            peaks = best if peaks is None else jnp.maximum(peaks, best)
            sums = factor if sums is None else sums + factor
        summed = jnp.dot(
            jnp.concatenate(factors, axis=1), block, preferred_element_type=jnp.float32
        )
        return peaks, sums, summed

    def stat_rows(peaks, sums):
        top = jnp.max(jnp.transpose(peaks), axis=0, keepdims=True)
        mass = jnp.sum(jnp.transpose(sums), axis=0, keepdims=True)
        return jnp.concatenate([top, mass], axis=0)

    def run(is_inner):
        me = 1 if is_inner else 0
        slots = 4 if is_inner else 3
        last = slots - 1
        own_rows = keys.at[me, 0]

        def z_copy(slot, target, part, device):
            ref = pl.ds(part * piece, piece)
            return remote(
                keys.at[slot, 0, ref], keys.at[target, 0, ref], z_send, z_recv.at[target, part],
                device,
            )

        def z_meta(slot, target, device):
            return remote(
                key_meta.at[slot, 0], key_meta.at[target, 0], zm_send, zm_recv.at[target], device
            )

        def c_copy(slot, part=None):
            ref = pl.ds(0, rows) if part is None else pl.ds(part * piece, piece)
            return remote(
                keys.at[slot, 0, ref], keys.at[slot, 1, ref], c_send, c_recv.at[slot], partner
            )

        def c_meta(slot):
            return remote(
                key_meta.at[slot, 0], key_meta.at[slot, 1], cm_send, cm_recv.at[slot], partner
            )

        def wait_partner(slot):
            arrived(key_meta.at[slot, 1], cm_recv.at[slot])
            arrived(keys.at[slot, 1], c_recv.at[slot])

        if is_inner:
            onward = {1: (2, far_device), 0: (3, far_device), 2: (1, end_device), 3: (2, end_device)}
        else:
            onward = {0: (0, next_device)}

        def take_meta(slot):
            arrived(key_meta.at[slot, 0], zm_recv.at[slot])
            if slot in onward:
                z_meta(slot, *onward[slot]).start()
            c_meta(slot).start()

        def take(slot, part):
            ref = keys.at[slot, 0, pl.ds(part * piece, piece)]
            arrived(ref, z_recv.at[slot, part])
            if slot in onward:
                target, device = onward[slot]
                z_copy(slot, target, part, device).start()
            c_copy(slot, part).start()

        def q_copy(source, spot, side, recv, device, send=1):
            return remote(
                source.at[halves[side]], plane.at[spot - 1, 0, halves[side]], q_send.at[send],
                q_recv.at[recv], device,
            )

        def q_arrived(spot, side, recv):
            arrived(plane.at[spot - 1, 0, halves[side]], q_recv.at[recv])

        def q_meta(source, spot, device):
            return remote(
                spot_meta.at[source], spot_meta.at[spot], qm_send, qm_recv.at[spot - 1], device
            )

        def q_meta_arrived(spot):
            arrived(spot_meta.at[spot], qm_recv.at[spot - 1])

        target, device = onward[me]
        z_meta(me, target, device).start()
        for part in range(PIECES):
            z_copy(me, target, part, device).start()
        q_meta(0, beside_x, x_device).start()
        q_meta(0, beside_y, y_device).start()
        q_copy(own_rows, beside_x, 0, 0, x_device, 0).start()
        q_copy(own_rows, beside_y, 1, 3, y_device, 0).start()
        c_meta(me).start()
        c_copy(me).start()
        query_col[0] = column(spot_meta[0, 0:1, :])
        sent(own_rows, q_send.at[0])
        q_copy(own_rows, beside_x, 1, 1, x_device).start()
        q_copy(own_rows, beside_y, 0, 2, y_device).start()

        def relay_q():
            q_meta_arrived(beside_x)
            q_meta(beside_x, corner, y_device).start()
            q_arrived(beside_x, 0, 0)
            q_copy(plane.at[beside_x - 1, 0], corner, 0, 4, y_device).start()
            q_meta_arrived(beside_y)
            q_arrived(beside_y, 1, 3)
            q_copy(plane.at[beside_y - 1, 0], corner, 1, 5, x_device).start()

        def pass_on(spot):
            if is_inner:
                remote(
                    plane.at[spot - 1, 0], plane.at[spot - 1, 1], f_send.at[0], f_recv.at[0], partner
                ).start()

        def finish_q(spot):
            if spot == beside_x:
                q_arrived(beside_x, 1, 1)
            elif spot == beside_y:
                q_arrived(beside_y, 0, 2)
            else:
                q_meta_arrived(corner)
                q_arrived(corner, 0, 4)
                q_arrived(corner, 1, 5)
                if is_inner:
                    remote(
                        spot_meta.at[1:SPOTS], plane_meta, f_send.at[1], f_recv.at[1], partner
                    ).start()
            pass_on(spot)
            query_col[spot] = column(spot_meta[spot, 0:1, :])

        def batch(spot, first, end):
            chosen = keys[me, 0] if spot == 0 else plane[spot - 1, 0]
            count = end - first
            itself = (me - first) * PAIR if spot == 0 and first <= me < end else None
            return terms(
                chosen,
                query_col[spot],
                keys[first:end].reshape(count * PAIR * rows, features),
                [key_meta[slot, side] for slot in range(first, end) for side in range(PAIR)],
                itself,
            )

        def early(spot):
            peak[spot], weight[spot], total[spot] = batch(spot, 0, last)

        if is_inner:
            take_meta(0)
            take_meta(2)
            for part in range(PIECES):
                take(0, part)
                take(2, part)
                if part == 0:
                    relay_q()
            wait_partner(me)
            wait_partner(0)
            finish_q(beside_x)
            finish_q(beside_y)
            wait_partner(2)
        else:
            relay_q()
            finish_q(beside_x)
            finish_q(beside_y)
            wait_partner(me)
            take_meta(1)
            for part in range(PIECES):
                take(1, part)
            wait_partner(1)
        if not is_inner:
            early(0)
        take_meta(last)
        todo = (beside_x, beside_y, corner)
        for part in range(PIECES):
            take(last, part)
            if part % (PIECES // 4) == 0 and part // (PIECES // 4) < len(todo):
                spot = todo[part // (PIECES // 4)]
                if spot == corner:
                    finish_q(corner)
                early(spot)
        if is_inner:
            early(0)

        def h_copies():
            return (
                remote(help_stat_out, help_stat_in, h_send.at[0], h_recv.at[0], end_device),
                remote(help_out, help_in, h_send.at[1], h_recv.at[1], end_device),
            )

        wait_partner(last)

        def p_copy(spot, side):
            return remote(
                part_out.at[spot - 1, halves[side]], part_in.at[spot - 1, halves[side]],
                p_send.at[1], p_recv, x_device if spot == beside_x else y_device,
            )

        def corner_copy(side):
            return remote(
                part_out.at[corner - 1, halves[side]], part_in.at[corner - 1, halves[side]],
                p_send.at[0], corner_recv.at[side], (x_device, y_device)[side],
            )

        def s_copy(spot, device, recv):
            return remote(stat_out.at[spot - 1], stat_in.at[spot - 1], s_send, recv, device)

        def final(spot):
            peaks, sums, summed = batch(spot, last, slots)
            return jnp.maximum(peak[spot], peaks), weight[spot] + sums, total[spot] + summed

        block = keys[last].reshape(PAIR * rows, features)
        metas = [key_meta[last, side] for side in range(PAIR)]
        others = plane[:, 0].reshape((SPOTS - 1) * rows, features)
        columns = query_col[1:SPOTS].reshape((SPOTS - 1) * rows, rows)
        peaks, sums, summed = terms(others, columns, block, metas, None)
        stats = {}
        for spot in (corner, beside_x, beside_y):
            of = slice((spot - 1) * rows, spot * rows)
            whole = total[spot] + summed[of]
            if spot == corner:
                part_out[spot - 1] = whole.astype(jnp.bfloat16)
                corner_copy(0).start()
                corner_copy(1).start()
            else:
                total[spot] = whole
            stats[spot] = stat_rows(jnp.maximum(peak[spot], peaks[of]), weight[spot] + sums[of])
            if spot != beside_y:
                stat_out[spot - 1] = stats[spot]
                s_copy(spot, x_device, sc_recv if spot == corner else s_recv).start()
        for spot, side in ((beside_x, 0), (beside_y, 1)):
            part_out[spot - 1, halves[side]] = total[spot, halves[side]].astype(jnp.bfloat16)
        peaks, sums, summed = final(0)
        own_stats = stat_rows(peaks, sums)
        total[0] = summed + keys[me, 0].astype(jnp.float32)

        if is_inner:
            for ref, index in ((plane_meta, 1), (plane.at[:, 1], 0)):
                arrived(ref, f_recv.at[index])
            chosen = keys[0, 0]
            buckets = column(key_meta[0, 0, 0:1, :])
            near = terms(
                chosen, buckets, keys[me].reshape(PAIR * rows, features),
                [key_meta[me, side] for side in range(PAIR)], None,
            )
            wider = terms(
                chosen, buckets, plane[...].reshape((SPOTS - 1) * PAIR * rows, features),
                [ref[spot] for spot in range(SPOTS - 1) for ref in (spot_meta.at[1:SPOTS], plane_meta)],
                None,
            )
            help_out[...] = (near[2] + wider[2]).astype(jnp.bfloat16)
            help_stat_out[...] = stat_rows(jnp.maximum(near[0], wider[0]), near[1] + wider[1])
            for copy in h_copies():
                copy.start()

        sent(part_out.at[corner - 1], p_send.at[0])
        for spot, side in ((beside_x, 0), (beside_y, 1)):
            p_copy(spot, side).start()
        arrived(stat_in.at[corner - 1], sc_recv)
        stat_out[beside_y - 1] = jnp.concatenate(
            [
                jnp.maximum(stats[beside_y][0:1], stat_in[corner - 1, 0:1]),
                stats[beside_y][1:2] + stat_in[corner - 1, 1:2],
            ],
            axis=0,
        )
        s_copy(beside_y, y_device, s_recv).start()
        for spot, side in ((beside_x, 1), (beside_y, 0)):
            arrived(part_in.at[corner - 1, halves[side]], corner_recv.at[side])
            part_out[spot - 1, halves[side]] = (
                total[spot, halves[side]] + part_in[corner - 1, halves[side]].astype(jnp.float32)
            ).astype(jnp.bfloat16)
            p_copy(spot, side).start()

        top, mass = own_stats[0:1], own_stats[1:2]
        if not is_inner:
            for copy in h_copies():
                copy.wait_recv()
            top = jnp.maximum(top, help_stat_in[0:1])
            mass = mass + help_stat_in[1:2]
            total[0] += help_in[...].astype(jnp.float32)
        arrived(stat_in.at[0 : corner - 1], s_recv)
        for spot in (beside_x, beside_y):
            top = jnp.maximum(top, stat_in[spot - 1, 0:1])
            mass = mass + stat_in[spot - 1, 1:2]
        best_ref[...] = top
        below = column(1.0 + mass)[:, 0:1]
        arrived(part_in.at[0 : corner - 1], p_recv)
        result = total[0]
        for spot in (beside_x, beside_y):
            result = result + part_in[spot - 1].astype(jnp.float32)
        mean_ref[...] = (result / below).astype(jnp.bfloat16)

        blocks = keys.at[0:slots, 0]
        metas = key_meta.at[0:slots, 0]
        sent(blocks if is_inner else keys.at[0, 0], z_send)
        sent(metas if is_inner else key_meta.at[0, 0], zm_send)
        sent(blocks, c_send)
        sent(metas, cm_send)
        sent(plane.at[0 : corner - 1, 0], q_send.at[1])
        sent(spot_meta.at[1:SPOTS], qm_send)
        sent(part_out.at[0 : corner - 1], p_send.at[1])
        sent(stat_out, s_send)
        if is_inner:
            sent(plane.at[:, 0], f_send.at[0])
            sent(plane_meta, f_send.at[1])
            for copy in h_copies():
                copy.wait_send()

    @pl.when(inner)
    def _():
        run(True)

    @pl.when(jnp.logical_not(inner))
    def _():
        run(False)


def finish_kernel(mean_ref, best_ref, mean_out, best_out, line, sem):
    line[...] = best_ref[0].astype(jnp.bfloat16)
    copies = [
        pltpu.make_async_copy(mean_ref, mean_out, sem.at[0]),
        pltpu.make_async_copy(line, best_out, sem.at[1]),
    ]
    for copy in copies:
        copy.start()
    for copy in copies:
        copy.wait()


def finish(mean, best):
    rows, features = mean.shape
    vmem = pl.BlockSpec(memory_space=pltpu.VMEM)
    hbm = pl.BlockSpec(memory_space=pltpu.HBM)
    return pl.pallas_call(
        finish_kernel,
        out_shape=(
            jax.ShapeDtypeStruct((rows, features), jnp.bfloat16),
            jax.ShapeDtypeStruct((rows,), jnp.bfloat16),
        ),
        in_specs=[vmem, vmem],
        out_specs=(hbm, hbm),
        scratch_shapes=[pltpu.VMEM((rows,), jnp.bfloat16), pltpu.SemaphoreType.DMA((2,))],
        compiler_params=pltpu.CompilerParams(vmem_limit_bytes=4_000_000),
    )(mean, best)


def dense(embeddings, bucket_ids, valid_rows):
    rows, features = embeddings.shape
    dma = pltpu.SemaphoreType.DMA
    vmem = pl.BlockSpec(memory_space=pltpu.VMEM)
    others = SPOTS - 1

    def bf16(*shape):
        return pltpu.VMEM((*shape, rows, features), jnp.bfloat16)

    def f32(*shape):
        return pltpu.VMEM(shape, jnp.float32)

    mean, best = pl.pallas_call(
        dense_kernel,
        out_shape=(
            jax.ShapeDtypeStruct((rows, features), jnp.bfloat16),
            jax.ShapeDtypeStruct((1, rows), jnp.float32),
        ),
        in_specs=[pl.BlockSpec(memory_space=pltpu.HBM)] * 3,
        out_specs=(vmem, vmem),
        scratch_shapes=[
            bf16(), pltpu.VMEM((1, rows), jnp.int32), pltpu.VMEM((1, rows), jnp.int32),
            bf16(PLANES, PAIR), f32(PLANES, PAIR, 2, rows), bf16(others, PAIR),
            f32(SPOTS, 2, rows), f32(others, 2, rows), f32(SPOTS, rows, rows),
            f32(SPOTS, rows, features), f32(SPOTS, rows, rows), f32(SPOTS, rows, rows),
            bf16(others), bf16(others), f32(others, 2, rows), f32(others, 2, rows),
            bf16(), bf16(), f32(2, rows), f32(2, rows),
            dma((3,)), dma, dma((PLANES, PIECES)), dma, dma((PLANES,)),
            dma, dma((PLANES,)), dma, dma((PLANES,)),
            dma((2,)), dma((6,)), dma, dma((others,)), dma((2,)), dma((2,)),
            dma((2,)), dma((2,)), dma, dma, dma, dma, dma((2,)), dma((2,)),
        ],
        compiler_params=pltpu.CompilerParams(
            collective_id=0, has_side_effects=True, vmem_limit_bytes=GRANT
        ),
    )(
        *[
            pltpu.with_memory_space_constraint(value, pltpu.HBM)
            for value in (embeddings, bucket_ids.reshape(1, rows), valid_rows.reshape(1, rows))
        ]
    )
    return finish(mean, best)


def on_device(embeddings, bucket_ids, slot_ids, valid_rows):
    rows = embeddings.shape[0]
    groups = lax.axis_size("wide")
    blocks = lax.axis_size("blk")
    bucket_work = blocks * (2 * rows) ** 2
    dense_work = groups * blocks * rows**2
    fits = groups % PAIR == 0 and groups == PLANES * PAIR and blocks == PAIR * PAIR and rows == 128
    if fits and dense_work <= 4 * bucket_work:
        return dense(embeddings, bucket_ids, valid_rows)
    return by_bucket(embeddings, bucket_ids, slot_ids, valid_rows)


def solution(mesh):
    in_specs = (
        P(("wide", "blk"), None),
        P(("wide", "blk")),
        P(("wide", "blk")),
        P(("wide", "blk")),
    )
    out_specs = (P(("wide", "blk"), None), P(("wide", "blk")))
    return jax.shard_map(
        on_device, mesh=mesh, in_specs=in_specs, out_specs=out_specs, check_vma=False
    )
```

time: 31.5 us -> 31.5 us (level)
  no operation moved by 1% of the time
where the time goes in v2:
time: 31.5 us; the launch traced here: 31.3 us
  Pallas kernels  30.7 us (97%)
  between operations  0.64 us (2%)
    pallas_call x1, Pallas kernels, dense(): pl.pallas_call(dense_kernel, out_shape=(jax.ShapeDtypeStruct((rows, featu...  30 us
    pallas_call x1, Pallas kernels, finish(): pl.pallas_call(finish_kernel, out_shape=(jax.ShapeDtypeStruct((rows, feat...  0.7 us

profile of v2, /device:TPU:0, one launch (start us, length us, event | category | flops | bytes accessed | tf_op | source)
XLA Modules:
  0.0 31.3 jit_solution(4885273054951275478)
XLA Ops:
  0.6 30.0 %shard_map.50 = (bf16[128,768]{1,0:T(8,128)(2,1)S(1)}, f32[1,128]{1,0:T(1,128)S(1)}) custom-call(bf16[128,768]{1,0:T(8,128)(2,1)} %emb_hbm.1, s32[1,128]{1,0:T(1,128)} %bitcast.2, s32[1,128]{1,0:T(1,128)} %bitcast.3), custom_call_target="tpu_custom_call" | custom-call | tf_op jit(solution)/shard_map/pallas_call | solution.py:578
  30.6 0.7 %shard_map.51 = (bf16[128,768]{1,0:T(8,128)(2,1)}, bf16[128]{0:T(256)(128)(2,1)}) custom-call(bf16[128,768]{1,0:T(8,128)(2,1)S(1)} %get-tuple-element.4.mean_ref, f32[1,128]{1,0:T(1,128)S(1)} %get-tuple-element.5.best_ref), custom_call_target="tpu_custom_call" | custom-call | tf_op jit(solution)/shard_map/pallas_call | solution.py:553

commit v3 on v2

--- a/solution.py
+++ b/solution.py
@@ -148,6 +148,8 @@
     end_device = at(jnp.where(lower, 0, PLANES - 1), y, x, core)
     next_device = at(jnp.where(lower, 1, PLANES - 2), y, x, core)
     far_device = at(across_z, y, x, core)
+    first_device = at(0, y, x, core)
+    top_device = at(PLANES - 1, y, x, core)
 
     def remote(source, target, send, recv, device):
         return pltpu.make_async_remote_copy(
@@ -187,6 +189,10 @@
     @pl.when(jnp.logical_not(inner))
     def _():
         greet(next_device)
+
+    @pl.when(z == 0)
+    def _():
+        greet(top_device)
 
     for load in loads:
         load.wait()
@@ -200,7 +206,7 @@
     key_meta[own, 0] = meta
     spot_meta[0] = meta
 
-    pl.semaphore_wait(barrier, jnp.where(inner, 5, 4))
+    pl.semaphore_wait(barrier, jnp.where(z > 0, 5, 4))
 
     def column(row):
         return jnp.transpose(jnp.broadcast_to(row, (rows, rows)))
@@ -234,9 +240,10 @@
         mass = jnp.sum(jnp.transpose(sums), axis=0, keepdims=True)
         return jnp.concatenate([top, mass], axis=0)
 
-    def run(is_inner):
+    def run(place):
+        is_inner = 0 < place < PLANES - 1
         me = 1 if is_inner else 0
-        slots = 4 if is_inner else 3
+        slots = (2, 4, 4, 3)[place]
         last = slots - 1
         own_rows = keys.at[me, 0]
 
@@ -268,7 +275,9 @@
             arrived(keys.at[slot, 1], c_recv.at[slot])
 
         if is_inner:
-            onward = {1: (2, far_device), 0: (3, far_device), 2: (1, end_device), 3: (2, end_device)}
+            onward = {1: (2, far_device), 0: (3, far_device), 2: (1, end_device)}
+            if place > 1:
+                onward[3] = (2, end_device)
         else:
             onward = {0: (0, next_device)}
 
@@ -328,7 +337,7 @@
             q_copy(plane.at[beside_y - 1, 0], corner, 1, 5, x_device).start()
 
         def pass_on(spot):
-            if is_inner:
+            if place > 0:
                 remote(
                     plane.at[spot - 1, 0], plane.at[spot - 1, 1], f_send.at[0], f_recv.at[0], partner
                 ).start()
@@ -342,7 +351,7 @@
                 q_meta_arrived(corner)
                 q_arrived(corner, 0, 4)
                 q_arrived(corner, 1, 5)
-                if is_inner:
+                if place > 0:
                     remote(
                         spot_meta.at[1:SPOTS], plane_meta, f_send.at[1], f_recv.at[1], partner
                     ).start()
@@ -364,47 +373,110 @@
         def early(spot):
             peak[spot], weight[spot], total[spot] = batch(spot, 0, last)
 
-        if is_inner:
-            take_meta(0)
-            take_meta(2)
-            for part in range(PIECES):
-                take(0, part)
-                take(2, part)
-                if part == 0:
-                    relay_q()
-            wait_partner(me)
-            wait_partner(0)
+        def h_copies(giver, taker):
+            return (
+                remote(help_stat_out, help_stat_in.at[giver], h_send.at[0], h_recv.at[giver, 0], taker),
+                remote(help_out, help_in.at[giver], h_send.at[1], h_recv.at[giver, 1], taker),
+            )
+
+        if place > 0:
+            helped = h_copies(0, end_device) if is_inner else h_copies(1, first_device)
+
+        def assist():
+            slot = 0 if is_inner else last
+            for ref, index in ((plane_meta, 1), (plane.at[:, 1], 0)):
+                arrived(ref, f_recv.at[index])
+            chosen = keys[slot, 0]
+            buckets = column(key_meta[slot, 0, 0:1, :])
+            near = terms(
+                chosen, buckets, keys[me].reshape(PAIR * rows, features),
+                [key_meta[me, side] for side in range(PAIR)], None,
+            )
+            wider = terms(
+                chosen, buckets, plane[...].reshape((SPOTS - 1) * PAIR * rows, features),
+                [ref[spot] for spot in range(SPOTS - 1) for ref in (spot_meta.at[1:SPOTS], plane_meta)],
+                None,
+            )
+            help_out[...] = (near[2] + wider[2]).astype(jnp.bfloat16)
+            help_stat_out[...] = stat_rows(jnp.maximum(near[0], wider[0]), near[1] + wider[1])
+            for copy in helped:
+                copy.start()
+
+        def take_all(*order):
+            for slot, part in order:
+                take(slot, part)
+
+        if place == 0:
+            relay_q()
             finish_q(beside_x)
             finish_q(beside_y)
-            wait_partner(2)
+            wait_partner(0)
+            for spot in (0, beside_x, beside_y):
+                early(spot)
+            take_meta(1)
+            take(1, 0)
+            finish_q(corner)
+            early(corner)
+            take_all((1, 1), (1, 2), (1, 3))
+        elif place == 1:
+            take_meta(0)
+            take(0, 0)
+            take_meta(2)
+            take_all((0, 1), (2, 0))
+            relay_q()
+            take_all((0, 2), (2, 1), (0, 3), (2, 2), (2, 3))
+            finish_q(beside_x)
+            finish_q(beside_y)
+            for slot in range(last):
+                wait_partner(slot)
+            early(0)
+            take_meta(3)
+            take(3, 0)
+            finish_q(corner)
+            assist()
+            take(3, 1)
+            early(beside_x)
+            take(3, 2)
+            early(beside_y)
+            take(3, 3)
+            early(corner)
+        elif place == 2:
+            take_meta(2)
+            take(2, 0)
+            take_meta(0)
+            take_all((2, 1), (0, 0), (2, 2))
+            relay_q()
+            take_all((0, 1), (2, 3))
+            take_meta(3)
+            take_all((3, 0), (0, 2), (3, 1), (0, 3), (3, 2))
+            finish_q(beside_x)
+            finish_q(beside_y)
+            for slot in range(last):
+                wait_partner(slot)
+            early(0)
+            take(3, 3)
+            early(beside_x)
+            early(beside_y)
+            finish_q(corner)
+            early(corner)
         else:
             relay_q()
             finish_q(beside_x)
             finish_q(beside_y)
-            wait_partner(me)
+            wait_partner(0)
             take_meta(1)
-            for part in range(PIECES):
-                take(1, part)
+            take_all((1, 0), (1, 1), (1, 2), (1, 3))
             wait_partner(1)
-        if not is_inner:
             early(0)
-        take_meta(last)
-        todo = (beside_x, beside_y, corner)
-        for part in range(PIECES):
-            take(last, part)
-            if part % (PIECES // 4) == 0 and part // (PIECES // 4) < len(todo):
-                spot = todo[part // (PIECES // 4)]
-                if spot == corner:
-                    finish_q(corner)
-                early(spot)
-        if is_inner:
-            early(0)
-
-        def h_copies():
-            return (
-                remote(help_stat_out, help_stat_in, h_send.at[0], h_recv.at[0], end_device),
-                remote(help_out, help_in, h_send.at[1], h_recv.at[1], end_device),
-            )
+            early(beside_x)
+            take_meta(2)
+            take(2, 0)
+            early(beside_y)
+            take(2, 1)
+            finish_q(corner)
+            early(corner)
+            take_all((2, 2), (2, 3))
+            assist()
 
         wait_partner(last)
 
@@ -452,25 +524,8 @@
         own_stats = stat_rows(peaks, sums)
         total[0] = summed + keys[me, 0].astype(jnp.float32)
 
-        if is_inner:
-            for ref, index in ((plane_meta, 1), (plane.at[:, 1], 0)):
-                arrived(ref, f_recv.at[index])
-            chosen = keys[0, 0]
-            buckets = column(key_meta[0, 0, 0:1, :])
-            near = terms(
-                chosen, buckets, keys[me].reshape(PAIR * rows, features),
-                [key_meta[me, side] for side in range(PAIR)], None,
-            )
-            wider = terms(
-                chosen, buckets, plane[...].reshape((SPOTS - 1) * PAIR * rows, features),
-                [ref[spot] for spot in range(SPOTS - 1) for ref in (spot_meta.at[1:SPOTS], plane_meta)],
-                None,
-            )
-            help_out[...] = (near[2] + wider[2]).astype(jnp.bfloat16)
-            help_stat_out[...] = stat_rows(jnp.maximum(near[0], wider[0]), near[1] + wider[1])
-            for copy in h_copies():
-                copy.start()
-
+        if place == 2:
+            assist()
         sent(part_out.at[corner - 1], p_send.at[0])
         for spot, side in ((beside_x, 0), (beside_y, 1)):
             p_copy(spot, side).start()
@@ -491,12 +546,12 @@
             p_copy(spot, side).start()
 
         top, mass = own_stats[0:1], own_stats[1:2]
-        if not is_inner:
-            for copy in h_copies():
+        for giver in {0: (0, 1), 3: (0,)}.get(place, ()):
+            for copy in h_copies(giver, partner):
                 copy.wait_recv()
-            top = jnp.maximum(top, help_stat_in[0:1])
-            mass = mass + help_stat_in[1:2]
-            total[0] += help_in[...].astype(jnp.float32)
+            top = jnp.maximum(top, help_stat_in[giver, 0:1])
+            mass = mass + help_stat_in[giver, 1:2]
+            total[0] += help_in[giver].astype(jnp.float32)
         arrived(stat_in.at[0 : corner - 1], s_recv)
         for spot in (beside_x, beside_y):
             top = jnp.maximum(top, stat_in[spot - 1, 0:1])
@@ -511,27 +566,22 @@
 
         blocks = keys.at[0:slots, 0]
         metas = key_meta.at[0:slots, 0]
-        sent(blocks if is_inner else keys.at[0, 0], z_send)
-        sent(metas if is_inner else key_meta.at[0, 0], zm_send)
+        sent(keys.at[0 : len(onward), 0], z_send)
+        sent(key_meta.at[0 : len(onward), 0], zm_send)
         sent(blocks, c_send)
         sent(metas, cm_send)
         sent(plane.at[0 : corner - 1, 0], q_send.at[1])
         sent(spot_meta.at[1:SPOTS], qm_send)
         sent(part_out.at[0 : corner - 1], p_send.at[1])
         sent(stat_out, s_send)
-        if is_inner:
+        if place > 0:
             sent(plane.at[:, 0], f_send.at[0])
             sent(plane_meta, f_send.at[1])
-            for copy in h_copies():
+            for copy in helped:
                 copy.wait_send()
 
-    @pl.when(inner)
-    def _():
-        run(True)
-
-    @pl.when(jnp.logical_not(inner))
-    def _():
-        run(False)
+    for place in range(PLANES):
+        pl.when(z == place)(functools.partial(run, place))
 
 
 def finish_kernel(mean_ref, best_ref, mean_out, best_out, line, sem):
@@ -589,11 +639,11 @@
             f32(SPOTS, 2, rows), f32(others, 2, rows), f32(SPOTS, rows, rows),
             f32(SPOTS, rows, features), f32(SPOTS, rows, rows), f32(SPOTS, rows, rows),
             bf16(others), bf16(others), f32(others, 2, rows), f32(others, 2, rows),
-            bf16(), bf16(), f32(2, rows), f32(2, rows),
+            bf16(), bf16(2), f32(2, rows), f32(2, 2, rows),
             dma((3,)), dma, dma((PLANES, PIECES)), dma, dma((PLANES,)),
             dma, dma((PLANES,)), dma, dma((PLANES,)),
             dma((2,)), dma((6,)), dma, dma((others,)), dma((2,)), dma((2,)),
-            dma((2,)), dma((2,)), dma, dma, dma, dma, dma((2,)), dma((2,)),
+            dma((2,)), dma((2,)), dma, dma, dma, dma, dma((2,)), dma((2, 2)),
         ],
         compiler_params=pltpu.CompilerParams(
             collective_id=0, has_side_effects=True, vmem_limit_bytes=GRANT

time: 31.5 us -> 28.2 us (0.90)
  Pallas kernels: 30.7 us -> 27.3 us
    pallas_call x1, Pallas kernels: 30 us -> 26.6 us  [dense(): pl.pallas_call(dense_kernel, out_shape=(jax.ShapeDtypeStruct((rows, featu...]
where the time goes in v3:
time: 28.2 us; the launch traced here: 28.1 us
  Pallas kernels  27.3 us (97%)
  between operations  0.8 us (3%)
    pallas_call x1, Pallas kernels, dense(): pl.pallas_call(dense_kernel, out_shape=(jax.ShapeDtypeStruct((rows, featu...  26.6 us
    pallas_call x1, Pallas kernels, finish(): pl.pallas_call(finish_kernel, out_shape=(jax.ShapeDtypeStruct((rows, feat...  0.7 us

profile of v3, /device:TPU:0, one launch (start us, length us, event | category | flops | bytes accessed | tf_op | source)
XLA Modules:
  0.0 28.1 jit_solution(7611505245672135233)
XLA Ops:
  0.6 26.6 %shard_map.50 = (bf16[128,768]{1,0:T(8,128)(2,1)S(1)}, f32[1,128]{1,0:T(1,128)S(1)}) custom-call(bf16[128,768]{1,0:T(8,128)(2,1)} %emb_hbm.1, s32[1,128]{1,0:T(1,128)} %bitcast.2, s32[1,128]{1,0:T(1,128)} %bitcast.3), custom_call_target="tpu_custom_call" | custom-call | tf_op jit(solution)/shard_map/pallas_call | solution.py:628
  27.2 0.7 %shard_map.51 = (bf16[128,768]{1,0:T(8,128)(2,1)}, bf16[128]{0:T(256)(128)(2,1)}) custom-call(bf16[128,768]{1,0:T(8,128)(2,1)S(1)} %get-tuple-element.4.mean_ref, f32[1,128]{1,0:T(1,128)S(1)} %get-tuple-element.5.best_ref), custom_call_target="tpu_custom_call" | custom-call | tf_op jit(solution)/shard_map/pallas_call | solution.py:603

commit v4 on v3

--- a/solution.py
+++ b/solution.py
@@ -122,14 +122,14 @@
     emb_hbm, bucket_hbm, valid_hbm, mean_ref, best_ref,
     emb_ref, bucket_ref, valid_ref,
     keys, key_meta, plane, spot_meta, plane_meta, query_col, total, peak, weight,
-    part_out, part_in, stat_out, stat_in, help_out, help_in, help_stat_out, help_stat_in,
+    part_out, part_in, stat_out, stat_in, help_terms, help_out, help_in, help_stat_out, help_stat_in,
     load_sem, z_send, z_recv, zm_send, zm_recv, c_send, c_recv, cm_send, cm_recv,
     q_send, q_recv, qm_send, qm_recv, f_send, f_recv,
     p_send, corner_recv, p_recv, s_send, sc_recv, s_recv, h_send, h_recv,
 ):
     rows, features = emb_ref.shape
     piece = rows // PIECES
-    half = rows // 2
+    half, quarter = rows // 2, rows // 4
     halves = (pl.ds(0, half), pl.ds(half, half))
     wide, blk = lax.axis_index("wide"), lax.axis_index("blk")
     z, y = lax.div(wide, PAIR), lax.rem(wide, PAIR)
@@ -243,7 +243,7 @@
     def run(place):
         is_inner = 0 < place < PLANES - 1
         me = 1 if is_inner else 0
-        slots = (2, 4, 4, 3)[place]
+        slots = (3, 4, 4, 3)[place]
         last = slots - 1
         own_rows = keys.at[me, 0]
 
@@ -274,24 +274,23 @@
             arrived(key_meta.at[slot, 1], cm_recv.at[slot])
             arrived(keys.at[slot, 1], c_recv.at[slot])
 
-        if is_inner:
-            onward = {1: (2, far_device), 0: (3, far_device), 2: (1, end_device)}
-            if place > 1:
-                onward[3] = (2, end_device)
-        else:
-            onward = {0: (0, next_device)}
+        onward = {
+            0: {0: [(0, next_device)]},
+            1: {1: [(2, far_device), (1, end_device)], 0: [(3, far_device)], 2: [(2, end_device)]},
+            2: {1: [(2, far_device)], 0: [(3, far_device)], 2: [(1, end_device)], 3: [(2, end_device)]},
+            3: {0: [(0, next_device)]},
+        }[place]
 
         def take_meta(slot):
             arrived(key_meta.at[slot, 0], zm_recv.at[slot])
-            if slot in onward:
-                z_meta(slot, *onward[slot]).start()
+            for target, device in onward.get(slot, ()):
+                z_meta(slot, target, device).start()
             c_meta(slot).start()
 
         def take(slot, part):
             ref = keys.at[slot, 0, pl.ds(part * piece, piece)]
             arrived(ref, z_recv.at[slot, part])
-            if slot in onward:
-                target, device = onward[slot]
+            for target, device in onward.get(slot, ()):
                 z_copy(slot, target, part, device).start()
             c_copy(slot, part).start()
 
@@ -312,10 +311,11 @@
         def q_meta_arrived(spot):
             arrived(spot_meta.at[spot], qm_recv.at[spot - 1])
 
-        target, device = onward[me]
-        z_meta(me, target, device).start()
+        for target, device in onward[me]:
+            z_meta(me, target, device).start()
         for part in range(PIECES):
-            z_copy(me, target, part, device).start()
+            for target, device in onward[me]:
+                z_copy(me, target, part, device).start()
         q_meta(0, beside_x, x_device).start()
         q_meta(0, beside_y, y_device).start()
         q_copy(own_rows, beside_x, 0, 0, x_device, 0).start()
@@ -337,7 +337,7 @@
             q_copy(plane.at[beside_y - 1, 0], corner, 1, 5, x_device).start()
 
         def pass_on(spot):
-            if place > 0:
+            if place > 1:
                 remote(
                     plane.at[spot - 1, 0], plane.at[spot - 1, 1], f_send.at[0], f_recv.at[0], partner
                 ).start()
@@ -351,7 +351,7 @@
                 q_meta_arrived(corner)
                 q_arrived(corner, 0, 4)
                 q_arrived(corner, 1, 5)
-                if place > 0:
+                if place > 1:
                     remote(
                         spot_meta.at[1:SPOTS], plane_meta, f_send.at[1], f_recv.at[1], partner
                     ).start()
@@ -373,21 +373,49 @@
         def early(spot):
             peak[spot], weight[spot], total[spot] = batch(spot, 0, last)
 
-        def h_copies(giver, taker):
-            return (
-                remote(help_stat_out, help_stat_in.at[giver], h_send.at[0], h_recv.at[giver, 0], taker),
-                remote(help_out, help_in.at[giver], h_send.at[1], h_recv.at[giver, 1], taker),
-            )
-
-        if place > 0:
-            helped = h_copies(0, end_device) if is_inner else h_copies(1, first_device)
-
-        def assist():
+        def joint(first, end):
+            block = keys[first:end].reshape((end - first) * PAIR * rows, features)
+            metas = [key_meta[slot, side] for slot in range(first, end) for side in range(PAIR)]
+
+            def of(begin, stop):
+                count = (stop - begin) * rows
+                shape = (stop - begin, rows)
+                peaks, sums, summed = terms(
+                    plane[begin - 1 : stop - 1, 0].reshape(count, features),
+                    query_col[begin:stop].reshape(count, rows),
+                    block, metas, None,
+                )
+                return (
+                    peaks.reshape(*shape, rows), sums.reshape(*shape, rows),
+                    summed.reshape(*shape, features),
+                )
+
+            return of
+
+        def early_others():
+            peak[1:SPOTS], weight[1:SPOTS], total[1:SPOTS] = joint(0, last)(1, SPOTS)
+
+        def h_copy(side):
+            ref = halves[side]
+            return remote(
+                help_out.at[ref], help_in.at[ref], h_send.at[0], h_recv.at[0],
+                end_device if is_inner else first_device,
+            )
+
+        def h_stat():
+            return remote(
+                help_stat_out, help_stat_in, h_send.at[1], h_recv.at[1],
+                end_device if is_inner else first_device,
+            )
+
+        def assist(sides=(0, 1)):
             slot = 0 if is_inner else last
-            for ref, index in ((plane_meta, 1), (plane.at[:, 1], 0)):
-                arrived(ref, f_recv.at[index])
-            chosen = keys[slot, 0]
-            buckets = column(key_meta[slot, 0, 0:1, :])
+            if 0 in sides:
+                for ref, index in ((plane_meta, 1), (plane.at[:, 1], 0)):
+                    arrived(ref, f_recv.at[index])
+            of = slice(sides[0] * half, (sides[-1] + 1) * half)
+            chosen = keys[slot, 0, of]
+            buckets = column(key_meta[slot, 0, 0:1, :])[of]
             near = terms(
                 chosen, buckets, keys[me].reshape(PAIR * rows, features),
                 [key_meta[me, side] for side in range(PAIR)], None,
@@ -397,10 +425,14 @@
                 [ref[spot] for spot in range(SPOTS - 1) for ref in (spot_meta.at[1:SPOTS], plane_meta)],
                 None,
             )
-            help_out[...] = (near[2] + wider[2]).astype(jnp.bfloat16)
-            help_stat_out[...] = stat_rows(jnp.maximum(near[0], wider[0]), near[1] + wider[1])
-            for copy in helped:
-                copy.start()
+            help_out[of] = (near[2] + wider[2]).astype(jnp.bfloat16)
+            help_terms[0, of] = jnp.maximum(near[0], wider[0])
+            help_terms[1, of] = near[1] + wider[1]
+            for side in sides:
+                h_copy(side).start()
+            if 1 in sides:
+                help_stat_out[...] = stat_rows(help_terms[0], help_terms[1])
+                h_stat().start()
 
         def take_all(*order):
             for slot, part in order:
@@ -408,16 +440,18 @@
 
         if place == 0:
             relay_q()
+            take_meta(1)
+            take_all((1, 0), (1, 1), (1, 2), (1, 3))
             finish_q(beside_x)
             finish_q(beside_y)
             wait_partner(0)
-            for spot in (0, beside_x, beside_y):
-                early(spot)
-            take_meta(1)
-            take(1, 0)
+            wait_partner(1)
+            early(0)
+            take_meta(2)
+            take(2, 0)
             finish_q(corner)
-            early(corner)
-            take_all((1, 1), (1, 2), (1, 3))
+            early_others()
+            take_all((2, 1), (2, 2), (2, 3))
         elif place == 1:
             take_meta(0)
             take(0, 0)
@@ -433,31 +467,23 @@
             take_meta(3)
             take(3, 0)
             finish_q(corner)
-            assist()
-            take(3, 1)
-            early(beside_x)
-            take(3, 2)
-            early(beside_y)
-            take(3, 3)
-            early(corner)
+            early_others()
+            take_all((3, 1), (3, 2), (3, 3))
         elif place == 2:
             take_meta(2)
             take(2, 0)
             take_meta(0)
             take_all((2, 1), (0, 0), (2, 2))
             relay_q()
-            take_all((0, 1), (2, 3))
+            take_all((0, 1), (2, 3), (0, 2))
             take_meta(3)
-            take_all((3, 0), (0, 2), (3, 1), (0, 3), (3, 2))
+            take_all((3, 0), (0, 3), (3, 1), (3, 2))
             finish_q(beside_x)
             finish_q(beside_y)
             for slot in range(last):
                 wait_partner(slot)
-            early(0)
+            finish_q(corner)
             take(3, 3)
-            early(beside_x)
-            early(beside_y)
-            finish_q(corner)
             early(corner)
         else:
             relay_q()
@@ -466,16 +492,12 @@
             wait_partner(0)
             take_meta(1)
             take_all((1, 0), (1, 1), (1, 2), (1, 3))
+            finish_q(corner)
             wait_partner(1)
             early(0)
-            early(beside_x)
+            early_others()
             take_meta(2)
-            take(2, 0)
-            early(beside_y)
-            take(2, 1)
-            finish_q(corner)
-            early(corner)
-            take_all((2, 2), (2, 3))
+            take_all((2, 0), (2, 1), (2, 2), (2, 3))
             assist()
 
         wait_partner(last)
@@ -486,54 +508,71 @@
                 p_send.at[1], p_recv, x_device if spot == beside_x else y_device,
             )
 
-        def corner_copy(side):
-            return remote(
-                part_out.at[corner - 1, halves[side]], part_in.at[corner - 1, halves[side]],
-                p_send.at[0], corner_recv.at[side], (x_device, y_device)[side],
+        def corner_copy(side, turn):
+            ref = pl.ds(side * half + turn * quarter, quarter)
+            return remote(
+                part_out.at[corner - 1, ref], part_in.at[corner - 1, ref],
+                p_send.at[2 * turn], corner_recv.at[side], (x_device, y_device)[side],
             )
 
         def s_copy(spot, device, recv):
             return remote(stat_out.at[spot - 1], stat_in.at[spot - 1], s_send, recv, device)
 
+        begun = (corner,) if place == 2 else (0, 1, 2, 3)
+
         def final(spot):
+            if spot not in begun:
+                return batch(spot, 0, slots)
             peaks, sums, summed = batch(spot, last, slots)
             return jnp.maximum(peak[spot], peaks), weight[spot] + sums, total[spot] + summed
 
-        block = keys[last].reshape(PAIR * rows, features)
-        metas = [key_meta[last, side] for side in range(PAIR)]
-        others = plane[:, 0].reshape((SPOTS - 1) * rows, features)
-        columns = query_col[1:SPOTS].reshape((SPOTS - 1) * rows, rows)
-        peaks, sums, summed = terms(others, columns, block, metas, None)
-        stats = {}
-        for spot in (corner, beside_x, beside_y):
-            of = slice((spot - 1) * rows, spot * rows)
-            whole = total[spot] + summed[of]
-            if spot == corner:
-                part_out[spot - 1] = whole.astype(jnp.bfloat16)
-                corner_copy(0).start()
-                corner_copy(1).start()
+        def send_stats(spot, peaks, sums):
+            stat_out[spot - 1] = stat_rows(peaks, sums)
+            s_copy(spot, x_device, sc_recv if spot == corner else s_recv).start()
+
+        peaks, sums, summed = final(corner)
+        part_out[corner - 1] = summed.astype(jnp.bfloat16)
+        for turn in range(2):
+            for side in range(2):
+                corner_copy(side, turn).start()
+        send_stats(corner, peaks, sums)
+        both = (beside_x, beside_y)
+        if place != 2:
+            peaks, sums, summed = joint(last, slots)(1, 3)
+            finals = [
+                (
+                    jnp.maximum(peak[spot], peaks[spot - 1]), weight[spot] + sums[spot - 1],
+                    total[spot] + summed[spot - 1],
+                )
+                for spot in both
+            ]
+        else:
+            finals = [final(spot) for spot in both]
+        for spot, side, (peaks, sums, summed) in zip(both, (0, 1), finals):
+            total[spot] = summed
+            part_out[spot - 1, halves[side]] = summed[side * half : (side + 1) * half].astype(jnp.bfloat16)
+            if spot == beside_x:
+                send_stats(spot, peaks, sums)
             else:
-                total[spot] = whole
-            stats[spot] = stat_rows(jnp.maximum(peak[spot], peaks[of]), weight[spot] + sums[of])
-            if spot != beside_y:
-                stat_out[spot - 1] = stats[spot]
-                s_copy(spot, x_device, sc_recv if spot == corner else s_recv).start()
-        for spot, side in ((beside_x, 0), (beside_y, 1)):
-            part_out[spot - 1, halves[side]] = total[spot, halves[side]].astype(jnp.bfloat16)
-        peaks, sums, summed = final(0)
-        own_stats = stat_rows(peaks, sums)
-        total[0] = summed + keys[me, 0].astype(jnp.float32)
-
+                y_stats = stat_rows(peaks, sums)
+        def own_final():
+            peaks, sums, summed = final(0)
+            total[0] = summed + keys[me, 0].astype(jnp.float32)
+            return stat_rows(peaks, sums)
+
+        if place != 2:
+            own_stats = own_final()
+        sent(part_out.at[corner - 1, halves[0]], p_send.at[0])
+        for spot, side in zip(both, (0, 1)):
+            p_copy(spot, side).start()
         if place == 2:
+            own_stats = own_final()
             assist()
-        sent(part_out.at[corner - 1], p_send.at[0])
-        for spot, side in ((beside_x, 0), (beside_y, 1)):
-            p_copy(spot, side).start()
         arrived(stat_in.at[corner - 1], sc_recv)
         stat_out[beside_y - 1] = jnp.concatenate(
             [
-                jnp.maximum(stats[beside_y][0:1], stat_in[corner - 1, 0:1]),
-                stats[beside_y][1:2] + stat_in[corner - 1, 1:2],
+                jnp.maximum(y_stats[0:1], stat_in[corner - 1, 0:1]),
+                y_stats[1:2] + stat_in[corner - 1, 1:2],
             ],
             axis=0,
         )
@@ -546,12 +585,12 @@
             p_copy(spot, side).start()
 
         top, mass = own_stats[0:1], own_stats[1:2]
-        for giver in {0: (0, 1), 3: (0,)}.get(place, ()):
-            for copy in h_copies(giver, partner):
-                copy.wait_recv()
-            top = jnp.maximum(top, help_stat_in[giver, 0:1])
-            mass = mass + help_stat_in[giver, 1:2]
-            total[0] += help_in[giver].astype(jnp.float32)
+        if not is_inner:
+            arrived(help_stat_in, h_recv.at[1])
+            arrived(help_in, h_recv.at[0])
+            top = jnp.maximum(top, help_stat_in[0:1])
+            mass = mass + help_stat_in[1:2]
+            total[0] += help_in[...].astype(jnp.float32)
         arrived(stat_in.at[0 : corner - 1], s_recv)
         for spot in (beside_x, beside_y):
             top = jnp.maximum(top, stat_in[spot - 1, 0:1])
@@ -566,19 +605,21 @@
 
         blocks = keys.at[0:slots, 0]
         metas = key_meta.at[0:slots, 0]
-        sent(keys.at[0 : len(onward), 0], z_send)
-        sent(key_meta.at[0 : len(onward), 0], zm_send)
+        hops = sum(len(ways) for ways in onward.values())
+        sent(keys.at[0:hops, 0], z_send)
+        sent(key_meta.at[0:hops, 0], zm_send)
         sent(blocks, c_send)
         sent(metas, cm_send)
         sent(plane.at[0 : corner - 1, 0], q_send.at[1])
         sent(spot_meta.at[1:SPOTS], qm_send)
         sent(part_out.at[0 : corner - 1], p_send.at[1])
+        sent(part_out.at[corner - 1, halves[0]], p_send.at[2])
         sent(stat_out, s_send)
-        if place > 0:
+        if place > 1:
             sent(plane.at[:, 0], f_send.at[0])
             sent(plane_meta, f_send.at[1])
-            for copy in helped:
-                copy.wait_send()
+            sent(help_out, h_send.at[0])
+            sent(help_stat_out, h_send.at[1])
 
     for place in range(PLANES):
         pl.when(z == place)(functools.partial(run, place))
@@ -639,11 +680,11 @@
             f32(SPOTS, 2, rows), f32(others, 2, rows), f32(SPOTS, rows, rows),
             f32(SPOTS, rows, features), f32(SPOTS, rows, rows), f32(SPOTS, rows, rows),
             bf16(others), bf16(others), f32(others, 2, rows), f32(others, 2, rows),
-            bf16(), bf16(2), f32(2, rows), f32(2, 2, rows),
+            f32(2, rows, rows), bf16(), bf16(), f32(2, rows), f32(2, rows),
             dma((3,)), dma, dma((PLANES, PIECES)), dma, dma((PLANES,)),
             dma, dma((PLANES,)), dma, dma((PLANES,)),
             dma((2,)), dma((6,)), dma, dma((others,)), dma((2,)), dma((2,)),
-            dma((2,)), dma((2,)), dma, dma, dma, dma, dma((2,)), dma((2, 2)),
+            dma((3,)), dma((2,)), dma, dma, dma, dma, dma((2,)), dma((2,)),
         ],
         compiler_params=pltpu.CompilerParams(
             collective_id=0, has_side_effects=True, vmem_limit_bytes=GRANT

time: 28.2 us -> 27.5 us (0.975)
  Pallas kernels: 27.3 us -> 26.5 us
    pallas_call x1, Pallas kernels: 26.6 us -> 25.8 us  [dense(): pl.pallas_call(dense_kernel, out_shape=(jax.ShapeDtypeStruct((rows, featu...]
where the time goes in v4:
time: 27.5 us; the launch traced here: 27.3 us
  Pallas kernels  26.5 us (96%)
  between operations  0.8 us (3%)
    pallas_call x1, Pallas kernels, dense(): pl.pallas_call(dense_kernel, out_shape=(jax.ShapeDtypeStruct((rows, featu...  25.8 us
    pallas_call x1, Pallas kernels, finish(): pl.pallas_call(finish_kernel, out_shape=(jax.ShapeDtypeStruct((rows, feat...  0.7 us

profile of v4, /device:TPU:0, one launch (start us, length us, event | category | flops | bytes accessed | tf_op | source)
XLA Modules:
  0.0 27.3 jit_solution(2005183940313720428)
XLA Ops:
  0.6 25.8 %shard_map.50 = (bf16[128,768]{1,0:T(8,128)(2,1)S(1)}, f32[1,128]{1,0:T(1,128)S(1)}) custom-call(bf16[128,768]{1,0:T(8,128)(2,1)} %emb_hbm.1, s32[1,128]{1,0:T(1,128)} %bitcast.2, s32[1,128]{1,0:T(1,128)} %bitcast.3), custom_call_target="tpu_custom_call" | custom-call | tf_op jit(solution)/shard_map/pallas_call | solution.py:669
  26.5 0.7 %shard_map.51 = (bf16[128,768]{1,0:T(8,128)(2,1)}, bf16[128]{0:T(256)(128)(2,1)}) custom-call(bf16[128,768]{1,0:T(8,128)(2,1)S(1)} %get-tuple-element.4.mean_ref, f32[1,128]{1,0:T(1,128)S(1)} %get-tuple-element.5.best_ref), custom_call_target="tpu_custom_call" | custom-call | tf_op jit(solution)/shard_map/pallas_call | solution.py:644

commit v5 on v4

--- a/solution.py
+++ b/solution.py
@@ -114,7 +114,7 @@
 PAIR = 2
 PLANES = 4
 SPOTS = PAIR * PAIR
-PIECES = 4
+PIECES = 8
 GRANT = 56_240_000
 
 
@@ -122,10 +122,10 @@
     emb_hbm, bucket_hbm, valid_hbm, mean_ref, best_ref,
     emb_ref, bucket_ref, valid_ref,
     keys, key_meta, plane, spot_meta, plane_meta, query_col, total, peak, weight,
-    part_out, part_in, stat_out, stat_in, help_terms, help_out, help_in, help_stat_out, help_stat_in,
-    load_sem, z_send, z_recv, zm_send, zm_recv, c_send, c_recv, cm_send, cm_recv,
-    q_send, q_recv, qm_send, qm_recv, f_send, f_recv,
-    p_send, corner_recv, p_recv, s_send, sc_recv, s_recv, h_send, h_recv,
+    part_out, part_in, stat_out, stat_in, help_out, help_in, help_stat_out, help_stat_in,
+    ready, load_sem, z_send, z_recv, zm_recv, c_send, c_recv, cm_recv,
+    q_send, q_recv, qm_recv, f_send, f_recv,
+    p_send, corner_recv, p_recv, sc_recv, s_recv, h_send, h_recv, small_send,
 ):
     rows, features = emb_ref.shape
     piece = rows // PIECES
@@ -181,14 +181,13 @@
     greet(y_device)
     greet(partner)
 
-    @pl.when(inner)
+    @pl.when(z < PLANES - 1)
     def _():
-        greet(far_device)
-        greet(end_device)
-
-    @pl.when(jnp.logical_not(inner))
+        greet(at(z + 1, y, x, core))
+
+    @pl.when(z == 1)
     def _():
-        greet(next_device)
+        greet(first_device)
 
     @pl.when(z == 0)
     def _():
@@ -206,7 +205,13 @@
     key_meta[own, 0] = meta
     spot_meta[0] = meta
 
-    pl.semaphore_wait(barrier, jnp.where(z > 0, 5, 4))
+    pl.semaphore_wait(barrier, jnp.where(z == PLANES - 1, 5, 4))
+
+    @pl.when(z >= 2)
+    def _():
+        pl.semaphore_signal(
+            ready, inc=1, device_id=at(z - 1, y, x, core), device_id_type=pl.DeviceIdType.MESH
+        )
 
     def column(row):
         return jnp.transpose(jnp.broadcast_to(row, (rows, rows)))
@@ -243,20 +248,20 @@
     def run(place):
         is_inner = 0 < place < PLANES - 1
         me = 1 if is_inner else 0
-        slots = (3, 4, 4, 3)[place]
+        slots = (3, 4, 3, 2)[place]
         last = slots - 1
         own_rows = keys.at[me, 0]
 
         def z_copy(slot, target, part, device):
             ref = pl.ds(part * piece, piece)
             return remote(
-                keys.at[slot, 0, ref], keys.at[target, 0, ref], z_send, z_recv.at[target, part],
+                keys.at[slot, 0, ref], keys.at[target, 0, ref], z_send, z_recv.at[(0, 1, 2, 1)[target], part],
                 device,
             )
 
         def z_meta(slot, target, device):
             return remote(
-                key_meta.at[slot, 0], key_meta.at[target, 0], zm_send, zm_recv.at[target], device
+                key_meta.at[slot, 0], key_meta.at[target, 0], small_send, zm_recv.at[target], device
             )
 
         def c_copy(slot, part=None):
@@ -267,7 +272,7 @@
 
         def c_meta(slot):
             return remote(
-                key_meta.at[slot, 0], key_meta.at[slot, 1], cm_send, cm_recv.at[slot], partner
+                key_meta.at[slot, 0], key_meta.at[slot, 1], small_send, cm_recv.at[slot], partner
             )
 
         def wait_partner(slot):
@@ -276,10 +281,17 @@
 
         onward = {
             0: {0: [(0, next_device)]},
-            1: {1: [(2, far_device), (1, end_device)], 0: [(3, far_device)], 2: [(2, end_device)]},
-            2: {1: [(2, far_device)], 0: [(3, far_device)], 2: [(1, end_device)], 3: [(2, end_device)]},
+            1: {1: [(1, end_device)], 0: [(2, far_device)], 2: [(2, end_device)]},
+            2: {1: [(2, far_device)], 0: [(3, far_device)], 2: [(1, end_device)]},
             3: {0: [(0, next_device)]},
         }[place]
+        helps = {
+            0: [],
+            1: [(2, far_device, 0), (3, top_device, 1)],
+            2: [(0, end_device, 0)],
+            3: [(1, first_device, 0)],
+        }[place]
+        helpers = (1, 0, 1, 2)[place]
 
         def take_meta(slot):
             arrived(key_meta.at[slot, 0], zm_recv.at[slot])
@@ -288,8 +300,12 @@
             c_meta(slot).start()
 
         def take(slot, part):
+            for step in range(PIECES // 4):
+                take_piece(slot, part * (PIECES // 4) + step)
+
+        def take_piece(slot, part):
             ref = keys.at[slot, 0, pl.ds(part * piece, piece)]
-            arrived(ref, z_recv.at[slot, part])
+            arrived(ref, z_recv.at[(0, 1, 2, 1)[slot], part])
             for target, device in onward.get(slot, ()):
                 z_copy(slot, target, part, device).start()
             c_copy(slot, part).start()
@@ -305,7 +321,7 @@
 
         def q_meta(source, spot, device):
             return remote(
-                spot_meta.at[source], spot_meta.at[spot], qm_send, qm_recv.at[spot - 1], device
+                spot_meta.at[source], spot_meta.at[spot], small_send, qm_recv.at[spot - 1], device
             )
 
         def q_meta_arrived(spot):
@@ -337,9 +353,9 @@
             q_copy(plane.at[beside_y - 1, 0], corner, 1, 5, x_device).start()
 
         def pass_on(spot):
-            if place > 1:
+            if place > 0:
                 remote(
-                    plane.at[spot - 1, 0], plane.at[spot - 1, 1], f_send.at[0], f_recv.at[0], partner
+                    plane.at[spot - 1, 0], plane.at[spot - 1, 1], f_send, f_recv.at[0], partner
                 ).start()
 
         def finish_q(spot):
@@ -351,9 +367,9 @@
                 q_meta_arrived(corner)
                 q_arrived(corner, 0, 4)
                 q_arrived(corner, 1, 5)
-                if place > 1:
+                if place > 0:
                     remote(
-                        spot_meta.at[1:SPOTS], plane_meta, f_send.at[1], f_recv.at[1], partner
+                        spot_meta.at[1:SPOTS], plane_meta, small_send, f_recv.at[1], partner
                     ).start()
             pass_on(spot)
             query_col[spot] = column(spot_meta[spot, 0:1, :])
@@ -395,27 +411,13 @@
         def early_others():
             peak[1:SPOTS], weight[1:SPOTS], total[1:SPOTS] = joint(0, last)(1, SPOTS)
 
-        def h_copy(side):
-            ref = halves[side]
-            return remote(
-                help_out.at[ref], help_in.at[ref], h_send.at[0], h_recv.at[0],
-                end_device if is_inner else first_device,
-            )
-
-        def h_stat():
-            return remote(
-                help_stat_out, help_stat_in, h_send.at[1], h_recv.at[1],
-                end_device if is_inner else first_device,
-            )
-
-        def assist(sides=(0, 1)):
-            slot = 0 if is_inner else last
-            if 0 in sides:
-                for ref, index in ((plane_meta, 1), (plane.at[:, 1], 0)):
-                    arrived(ref, f_recv.at[index])
-            of = slice(sides[0] * half, (sides[-1] + 1) * half)
-            chosen = keys[slot, 0, of]
-            buckets = column(key_meta[slot, 0, 0:1, :])[of]
+        def assist(turn):
+            slot, device, index = helps[turn]
+            if turn == 0:
+                arrived(plane_meta, f_recv.at[1])
+                arrived(plane.at[:, 1], f_recv.at[0])
+            chosen = keys[slot, 0]
+            buckets = column(key_meta[slot, 0, 0:1, :])
             near = terms(
                 chosen, buckets, keys[me].reshape(PAIR * rows, features),
                 [key_meta[me, side] for side in range(PAIR)], None,
@@ -425,14 +427,15 @@
                 [ref[spot] for spot in range(SPOTS - 1) for ref in (spot_meta.at[1:SPOTS], plane_meta)],
                 None,
             )
-            help_out[of] = (near[2] + wider[2]).astype(jnp.bfloat16)
-            help_terms[0, of] = jnp.maximum(near[0], wider[0])
-            help_terms[1, of] = near[1] + wider[1]
-            for side in sides:
-                h_copy(side).start()
-            if 1 in sides:
-                help_stat_out[...] = stat_rows(help_terms[0], help_terms[1])
-                h_stat().start()
+            help_out[turn] = (near[2] + wider[2]).astype(jnp.bfloat16)
+            remote(
+                help_out.at[turn], help_in.at[index], h_send, h_recv.at[index, 0], device
+            ).start()
+            help_stat_out[turn] = stat_rows(jnp.maximum(near[0], wider[0]), near[1] + wider[1])
+            remote(
+                help_stat_out.at[turn], help_stat_in.at[index], small_send, h_recv.at[index, 1],
+                device,
+            ).start()
 
         def take_all(*order):
             for slot, part in order:
@@ -453,6 +456,7 @@
             early_others()
             take_all((2, 1), (2, 2), (2, 3))
         elif place == 1:
+            pl.semaphore_wait(ready, 1)
             take_meta(0)
             take(0, 0)
             take_meta(2)
@@ -468,37 +472,34 @@
             take(3, 0)
             finish_q(corner)
             early_others()
-            take_all((3, 1), (3, 2), (3, 3))
+            take_all((3, 1), (3, 2))
+            assist(0)
+            take(3, 3)
         elif place == 2:
+            take_meta(0)
+            take(0, 0)
+            pl.semaphore_wait(ready, 1)
             take_meta(2)
-            take(2, 0)
-            take_meta(0)
-            take_all((2, 1), (0, 0), (2, 2))
             relay_q()
-            take_all((0, 1), (2, 3), (0, 2))
-            take_meta(3)
-            take_all((3, 0), (0, 3), (3, 1), (3, 2))
+            take_all((2, 0), (0, 1), (2, 1), (0, 2), (2, 2), (0, 3), (2, 3))
             finish_q(beside_x)
             finish_q(beside_y)
             for slot in range(last):
                 wait_partner(slot)
             finish_q(corner)
-            take(3, 3)
-            early(corner)
         else:
             relay_q()
             finish_q(beside_x)
             finish_q(beside_y)
             wait_partner(0)
             take_meta(1)
-            take_all((1, 0), (1, 1), (1, 2), (1, 3))
+            take(1, 0)
+            early(0)
+            take(1, 1)
             finish_q(corner)
-            wait_partner(1)
-            early(0)
             early_others()
-            take_meta(2)
-            take_all((2, 0), (2, 1), (2, 2), (2, 3))
-            assist()
+            take_all((1, 2), (1, 3))
+            assist(0)
 
         wait_partner(last)
 
@@ -516,9 +517,9 @@
             )
 
         def s_copy(spot, device, recv):
-            return remote(stat_out.at[spot - 1], stat_in.at[spot - 1], s_send, recv, device)
-
-        begun = (corner,) if place == 2 else (0, 1, 2, 3)
+            return remote(stat_out.at[spot - 1], stat_in.at[spot - 1], small_send, recv, device)
+
+        begun = () if place == 2 else (0, 1, 2, 3)
 
         def final(spot):
             if spot not in begun:
@@ -536,18 +537,16 @@
             for side in range(2):
                 corner_copy(side, turn).start()
         send_stats(corner, peaks, sums)
+        if place == 2:
+            assist(0)
         both = (beside_x, beside_y)
+        peaks, sums, summed = joint(0 if place == 2 else last, slots)(1, 3)
+        finals = [(peaks[index], sums[index], summed[index]) for index in range(2)]
         if place != 2:
-            peaks, sums, summed = joint(last, slots)(1, 3)
             finals = [
-                (
-                    jnp.maximum(peak[spot], peaks[spot - 1]), weight[spot] + sums[spot - 1],
-                    total[spot] + summed[spot - 1],
-                )
-                for spot in both
+                (jnp.maximum(peak[spot], top), weight[spot] + mass, total[spot] + whole)
+                for spot, (top, mass, whole) in zip(both, finals)
             ]
-        else:
-            finals = [final(spot) for spot in both]
         for spot, side, (peaks, sums, summed) in zip(both, (0, 1), finals):
             total[spot] = summed
             part_out[spot - 1, halves[side]] = summed[side * half : (side + 1) * half].astype(jnp.bfloat16)
@@ -560,14 +559,12 @@
             total[0] = summed + keys[me, 0].astype(jnp.float32)
             return stat_rows(peaks, sums)
 
-        if place != 2:
-            own_stats = own_final()
+        own_stats = own_final()
         sent(part_out.at[corner - 1, halves[0]], p_send.at[0])
         for spot, side in zip(both, (0, 1)):
             p_copy(spot, side).start()
-        if place == 2:
-            own_stats = own_final()
-            assist()
+        if place == 1:
+            assist(1)
         arrived(stat_in.at[corner - 1], sc_recv)
         stat_out[beside_y - 1] = jnp.concatenate(
             [
@@ -585,12 +582,12 @@
             p_copy(spot, side).start()
 
         top, mass = own_stats[0:1], own_stats[1:2]
-        if not is_inner:
-            arrived(help_stat_in, h_recv.at[1])
-            arrived(help_in, h_recv.at[0])
-            top = jnp.maximum(top, help_stat_in[0:1])
-            mass = mass + help_stat_in[1:2]
-            total[0] += help_in[...].astype(jnp.float32)
+        for index in range(helpers):
+            arrived(help_stat_in.at[index], h_recv.at[index, 1])
+            arrived(help_in.at[index], h_recv.at[index, 0])
+            top = jnp.maximum(top, help_stat_in[index, 0:1])
+            mass = mass + help_stat_in[index, 1:2]
+            total[0] += help_in[index].astype(jnp.float32)
         arrived(stat_in.at[0 : corner - 1], s_recv)
         for spot in (beside_x, beside_y):
             top = jnp.maximum(top, stat_in[spot - 1, 0:1])
@@ -603,23 +600,17 @@
             result = result + part_in[spot - 1].astype(jnp.float32)
         mean_ref[...] = (result / below).astype(jnp.bfloat16)
 
-        blocks = keys.at[0:slots, 0]
-        metas = key_meta.at[0:slots, 0]
         hops = sum(len(ways) for ways in onward.values())
         sent(keys.at[0:hops, 0], z_send)
-        sent(key_meta.at[0:hops, 0], zm_send)
-        sent(blocks, c_send)
-        sent(metas, cm_send)
+        sent(keys.at[0:slots, 0], c_send)
         sent(plane.at[0 : corner - 1, 0], q_send.at[1])
-        sent(spot_meta.at[1:SPOTS], qm_send)
         sent(part_out.at[0 : corner - 1], p_send.at[1])
         sent(part_out.at[corner - 1, halves[0]], p_send.at[2])
-        sent(stat_out, s_send)
-        if place > 1:
-            sent(plane.at[:, 0], f_send.at[0])
-            sent(plane_meta, f_send.at[1])
-            sent(help_out, h_send.at[0])
-            sent(help_stat_out, h_send.at[1])
+        pairs = hops + slots + 3 + 3 + (3 if place > 0 else 0) + len(helps)
+        sent(peak.at[0, pl.ds(0, 2 * pairs)], small_send)
+        if place > 0:
+            sent(plane.at[:, 0], f_send)
+            sent(help_out.at[0 : len(helps)], h_send)
 
     for place in range(PLANES):
         pl.when(z == place)(functools.partial(run, place))
@@ -680,11 +671,11 @@
             f32(SPOTS, 2, rows), f32(others, 2, rows), f32(SPOTS, rows, rows),
             f32(SPOTS, rows, features), f32(SPOTS, rows, rows), f32(SPOTS, rows, rows),
             bf16(others), bf16(others), f32(others, 2, rows), f32(others, 2, rows),
-            f32(2, rows, rows), bf16(), bf16(), f32(2, rows), f32(2, rows),
-            dma((3,)), dma, dma((PLANES, PIECES)), dma, dma((PLANES,)),
-            dma, dma((PLANES,)), dma, dma((PLANES,)),
-            dma((2,)), dma((6,)), dma, dma((others,)), dma((2,)), dma((2,)),
-            dma((3,)), dma((2,)), dma, dma, dma, dma, dma((2,)), dma((2,)),
+            bf16(2), bf16(2), f32(2, 2, rows), f32(2, 2, rows),
+            pltpu.SemaphoreType.REGULAR, dma((3,)), dma, dma((PLANES - 1, PIECES)), dma((PLANES,)),
+            dma, dma((PLANES,)), dma((PLANES,)),
+            dma((2,)), dma((6,)), dma((others,)), dma, dma((2,)),
+            dma((3,)), dma((2,)), dma, dma, dma, dma, dma((2, 2)), dma,
         ],
         compiler_params=pltpu.CompilerParams(
             collective_id=0, has_side_effects=True, vmem_limit_bytes=GRANT

time: 27.5 us -> 26.8 us (0.975)
  Pallas kernels: 26.5 us -> 25.8 us
    pallas_call x1, Pallas kernels: 25.8 us -> 25.1 us  [dense(): pl.pallas_call(dense_kernel, out_shape=(jax.ShapeDtypeStruct((rows, featu...]
where the time goes in v5:
time: 26.8 us; the launch traced here: 26.6 us
  Pallas kernels  25.8 us (96%)
  between operations  0.8 us (3%)
    pallas_call x1, Pallas kernels, dense(): pl.pallas_call(dense_kernel, out_shape=(jax.ShapeDtypeStruct((rows, featu...  25.1 us
    pallas_call x1, Pallas kernels, finish(): pl.pallas_call(finish_kernel, out_shape=(jax.ShapeDtypeStruct((rows, feat...  0.7 us

profile of v5, /device:TPU:0, one launch (start us, length us, event | category | flops | bytes accessed | tf_op | source)
XLA Modules:
  0.0 26.6 jit_solution(4103645550932058544)
XLA Ops:
  0.6 25.1 %shard_map.50 = (bf16[128,768]{1,0:T(8,128)(2,1)S(1)}, f32[1,128]{1,0:T(1,128)S(1)}) custom-call(bf16[128,768]{1,0:T(8,128)(2,1)} %emb_hbm.1, s32[1,128]{1,0:T(1,128)} %bitcast.2, s32[1,128]{1,0:T(1,128)} %bitcast.3), custom_call_target="tpu_custom_call" | custom-call | tf_op jit(solution)/shard_map/pallas_call | solution.py:660
  25.8 0.7 %shard_map.51 = (bf16[128,768]{1,0:T(8,128)(2,1)}, bf16[128]{0:T(256)(128)(2,1)}) custom-call(bf16[128,768]{1,0:T(8,128)(2,1)S(1)} %get-tuple-element.4.mean_ref, f32[1,128]{1,0:T(1,128)S(1)} %get-tuple-element.5.best_ref), custom_call_target="tpu_custom_call" | custom-call | tf_op jit(solution)/shard_map/pallas_call | solution.py:635

commit v6 on v5

--- a/solution.py
+++ b/solution.py
@@ -261,7 +261,7 @@
 
         def z_meta(slot, target, device):
             return remote(
-                key_meta.at[slot, 0], key_meta.at[target, 0], small_send, zm_recv.at[target], device
+                key_meta.at[slot, 0], key_meta.at[target, 0], small_send, zm_recv.at[(0, 1, 2, 1)[target]], device
             )
 
         def c_copy(slot, part=None):
@@ -294,7 +294,7 @@
         helpers = (1, 0, 1, 2)[place]
 
         def take_meta(slot):
-            arrived(key_meta.at[slot, 0], zm_recv.at[slot])
+            arrived(key_meta.at[slot, 0], zm_recv.at[(0, 1, 2, 1)[slot]])
             for target, device in onward.get(slot, ()):
                 z_meta(slot, target, device).start()
             c_meta(slot).start()
@@ -335,22 +335,22 @@
         q_meta(0, beside_x, x_device).start()
         q_meta(0, beside_y, y_device).start()
         q_copy(own_rows, beside_x, 0, 0, x_device, 0).start()
-        q_copy(own_rows, beside_y, 1, 3, y_device, 0).start()
+        q_copy(own_rows, beside_y, 1, 1, y_device, 0).start()
         c_meta(me).start()
         c_copy(me).start()
         query_col[0] = column(spot_meta[0, 0:1, :])
         sent(own_rows, q_send.at[0])
-        q_copy(own_rows, beside_x, 1, 1, x_device).start()
+        q_copy(own_rows, beside_x, 1, 2, x_device).start()
         q_copy(own_rows, beside_y, 0, 2, y_device).start()
 
         def relay_q():
             q_meta_arrived(beside_x)
             q_meta(beside_x, corner, y_device).start()
             q_arrived(beside_x, 0, 0)
-            q_copy(plane.at[beside_x - 1, 0], corner, 0, 4, y_device).start()
+            q_copy(plane.at[beside_x - 1, 0], corner, 0, 3, y_device).start()
             q_meta_arrived(beside_y)
-            q_arrived(beside_y, 1, 3)
-            q_copy(plane.at[beside_y - 1, 0], corner, 1, 5, x_device).start()
+            q_arrived(beside_y, 1, 1)
+            q_copy(plane.at[beside_y - 1, 0], corner, 1, 3, x_device).start()
 
         def pass_on(spot):
             if place > 0:
@@ -360,13 +360,10 @@
 
         def finish_q(spot):
             if spot == beside_x:
-                q_arrived(beside_x, 1, 1)
-            elif spot == beside_y:
-                q_arrived(beside_y, 0, 2)
-            else:
+                arrived(plane.at[beside_y - 1, 0], q_recv.at[2])
+            elif spot == corner:
                 q_meta_arrived(corner)
-                q_arrived(corner, 0, 4)
-                q_arrived(corner, 1, 5)
+                arrived(plane.at[corner - 1, 0], q_recv.at[3])
                 if place > 0:
                     remote(
                         spot_meta.at[1:SPOTS], plane_meta, small_send, f_recv.at[1], partner
@@ -472,9 +469,8 @@
             take(3, 0)
             finish_q(corner)
             early_others()
-            take_all((3, 1), (3, 2))
+            take_all((3, 1), (3, 2), (3, 3))
             assist(0)
-            take(3, 3)
         elif place == 2:
             take_meta(0)
             take(0, 0)
@@ -501,11 +497,24 @@
             take_all((1, 2), (1, 3))
             assist(0)
 
+        def one_side(side):
+            return terms(
+                plane[corner - 1, 0], query_col[corner], keys[last, side], [key_meta[last, side]], None
+            )
+
+        def corner_with(terms_of):
+            peaks, sums, summed = terms_of
+            return (
+                jnp.maximum(peak[corner], peaks), weight[corner] + sums, total[corner] + summed
+            )
+
+        if place == 0:
+            peak[corner], weight[corner], total[corner] = corner_with(one_side(0))
         wait_partner(last)
 
-        def p_copy(spot, side):
+        def p_copy(spot, ref):
             return remote(
-                part_out.at[spot - 1, halves[side]], part_in.at[spot - 1, halves[side]],
+                part_out.at[spot - 1, ref], part_in.at[spot - 1, ref],
                 p_send.at[1], p_recv, x_device if spot == beside_x else y_device,
             )
 
@@ -513,7 +522,7 @@
             ref = pl.ds(side * half + turn * quarter, quarter)
             return remote(
                 part_out.at[corner - 1, ref], part_in.at[corner - 1, ref],
-                p_send.at[2 * turn], corner_recv.at[side], (x_device, y_device)[side],
+                p_send.at[2 * turn], corner_recv.at[side, turn], (x_device, y_device)[side],
             )
 
         def s_copy(spot, device, recv):
@@ -531,7 +540,7 @@
             stat_out[spot - 1] = stat_rows(peaks, sums)
             s_copy(spot, x_device, sc_recv if spot == corner else s_recv).start()
 
-        peaks, sums, summed = final(corner)
+        peaks, sums, summed = corner_with(one_side(1)) if place == 0 else final(corner)
         part_out[corner - 1] = summed.astype(jnp.bfloat16)
         for turn in range(2):
             for side in range(2):
@@ -559,12 +568,15 @@
             total[0] = summed + keys[me, 0].astype(jnp.float32)
             return stat_rows(peaks, sums)
 
-        own_stats = own_final()
+        if place == 1:
+            assist(1)
+        else:
+            own_stats = own_final()
         sent(part_out.at[corner - 1, halves[0]], p_send.at[0])
         for spot, side in zip(both, (0, 1)):
-            p_copy(spot, side).start()
+            p_copy(spot, halves[side]).start()
         if place == 1:
-            assist(1)
+            own_stats = own_final()
         arrived(stat_in.at[corner - 1], sc_recv)
         stat_out[beside_y - 1] = jnp.concatenate(
             [
@@ -574,12 +586,14 @@
             axis=0,
         )
         s_copy(beside_y, y_device, s_recv).start()
-        for spot, side in ((beside_x, 1), (beside_y, 0)):
-            arrived(part_in.at[corner - 1, halves[side]], corner_recv.at[side])
-            part_out[spot - 1, halves[side]] = (
-                total[spot, halves[side]] + part_in[corner - 1, halves[side]].astype(jnp.float32)
-            ).astype(jnp.bfloat16)
-            p_copy(spot, side).start()
+        for turn in range(2):
+            for spot, side in ((beside_x, 1), (beside_y, 0)):
+                ref = pl.ds(side * half + turn * quarter, quarter)
+                arrived(part_in.at[corner - 1, ref], corner_recv.at[side, turn])
+                part_out[spot - 1, ref] = (
+                    total[spot, ref] + part_in[corner - 1, ref].astype(jnp.float32)
+                ).astype(jnp.bfloat16)
+                p_copy(spot, ref).start()
 
         top, mass = own_stats[0:1], own_stats[1:2]
         for index in range(helpers):
@@ -588,6 +602,17 @@
             top = jnp.maximum(top, help_stat_in[index, 0:1])
             mass = mass + help_stat_in[index, 1:2]
             total[0] += help_in[index].astype(jnp.float32)
+        hops = sum(len(ways) for ways in onward.values())
+        sent(keys.at[0:hops, 0], z_send)
+        sent(keys.at[0:slots, 0], c_send)
+        sent(plane.at[0 : corner - 1, 0], q_send.at[1])
+        sent(part_out.at[corner - 1, halves[0]], p_send.at[2])
+        pairs = hops + slots + 3 + 3 + (3 if place > 0 else 0) + len(helps)
+        sent(peak.at[0, pl.ds(0, 2 * pairs)], small_send)
+        if place > 0:
+            sent(plane.at[:, 0], f_send)
+            sent(help_out.at[0 : len(helps)], h_send)
+
         arrived(stat_in.at[0 : corner - 1], s_recv)
         for spot in (beside_x, beside_y):
             top = jnp.maximum(top, stat_in[spot - 1, 0:1])
@@ -600,17 +625,7 @@
             result = result + part_in[spot - 1].astype(jnp.float32)
         mean_ref[...] = (result / below).astype(jnp.bfloat16)
 
-        hops = sum(len(ways) for ways in onward.values())
-        sent(keys.at[0:hops, 0], z_send)
-        sent(keys.at[0:slots, 0], c_send)
-        sent(plane.at[0 : corner - 1, 0], q_send.at[1])
         sent(part_out.at[0 : corner - 1], p_send.at[1])
-        sent(part_out.at[corner - 1, halves[0]], p_send.at[2])
-        pairs = hops + slots + 3 + 3 + (3 if place > 0 else 0) + len(helps)
-        sent(peak.at[0, pl.ds(0, 2 * pairs)], small_send)
-        if place > 0:
-            sent(plane.at[:, 0], f_send)
-            sent(help_out.at[0 : len(helps)], h_send)
 
     for place in range(PLANES):
         pl.when(z == place)(functools.partial(run, place))
@@ -672,10 +687,10 @@
             f32(SPOTS, rows, features), f32(SPOTS, rows, rows), f32(SPOTS, rows, rows),
             bf16(others), bf16(others), f32(others, 2, rows), f32(others, 2, rows),
             bf16(2), bf16(2), f32(2, 2, rows), f32(2, 2, rows),
-            pltpu.SemaphoreType.REGULAR, dma((3,)), dma, dma((PLANES - 1, PIECES)), dma((PLANES,)),
+            pltpu.SemaphoreType.REGULAR, dma((3,)), dma, dma((PLANES - 1, PIECES)), dma((PLANES - 1,)),
             dma, dma((PLANES,)), dma((PLANES,)),
-            dma((2,)), dma((6,)), dma((others,)), dma, dma((2,)),
-            dma((3,)), dma((2,)), dma, dma, dma, dma, dma((2, 2)), dma,
+            dma((2,)), dma((4,)), dma((others,)), dma, dma((2,)),
+            dma((3,)), dma((2, 2)), dma, dma, dma, dma, dma((2, 2)), dma,
         ],
         compiler_params=pltpu.CompilerParams(
             collective_id=0, has_side_effects=True, vmem_limit_bytes=GRANT

time: 26.8 us -> 26.6 us (level)
  no operation moved by 1% of the time
where the time goes in v6:
time: 26.6 us; the launch traced here: 26.4 us
  Pallas kernels  25.6 us (96%)
  between operations  0.8 us (3%)
    pallas_call x1, Pallas kernels, dense(): pl.pallas_call(dense_kernel, out_shape=(jax.ShapeDtypeStruct((rows, featu...  24.9 us
    pallas_call x1, Pallas kernels, finish(): pl.pallas_call(finish_kernel, out_shape=(jax.ShapeDtypeStruct((rows, feat...  0.7 us

profile of v6, /device:TPU:0, one launch (start us, length us, event | category | flops | bytes accessed | tf_op | source)
XLA Modules:
  0.0 26.4 jit_solution(14980372442661496912)
XLA Ops:
  0.6 24.9 %shard_map.50 = (bf16[128,768]{1,0:T(8,128)(2,1)S(1)}, f32[1,128]{1,0:T(1,128)S(1)}) custom-call(bf16[128,768]{1,0:T(8,128)(2,1)} %emb_hbm.1, s32[1,128]{1,0:T(1,128)} %bitcast.2, s32[1,128]{1,0:T(1,128)} %bitcast.3), custom_call_target="tpu_custom_call" | custom-call | tf_op jit(solution)/shard_map/pallas_call | solution.py:675
  25.5 0.7 %shard_map.51 = (bf16[128,768]{1,0:T(8,128)(2,1)}, bf16[128]{0:T(256)(128)(2,1)}) custom-call(bf16[128,768]{1,0:T(8,128)(2,1)S(1)} %get-tuple-element.4.mean_ref, f32[1,128]{1,0:T(1,128)S(1)} %get-tuple-element.5.best_ref), custom_call_target="tpu_custom_call" | custom-call | tf_op jit(solution)/shard_map/pallas_call | solution.py:650

commit v7 on v6

--- a/solution.py
+++ b/solution.py
@@ -577,15 +577,6 @@
             p_copy(spot, halves[side]).start()
         if place == 1:
             own_stats = own_final()
-        arrived(stat_in.at[corner - 1], sc_recv)
-        stat_out[beside_y - 1] = jnp.concatenate(
-            [
-                jnp.maximum(y_stats[0:1], stat_in[corner - 1, 0:1]),
-                y_stats[1:2] + stat_in[corner - 1, 1:2],
-            ],
-            axis=0,
-        )
-        s_copy(beside_y, y_device, s_recv).start()
         for turn in range(2):
             for spot, side in ((beside_x, 1), (beside_y, 0)):
                 ref = pl.ds(side * half + turn * quarter, quarter)
@@ -594,6 +585,16 @@
                     total[spot, ref] + part_in[corner - 1, ref].astype(jnp.float32)
                 ).astype(jnp.bfloat16)
                 p_copy(spot, ref).start()
+            if turn == 0:
+                arrived(stat_in.at[corner - 1], sc_recv)
+                stat_out[beside_y - 1] = jnp.concatenate(
+                    [
+                        jnp.maximum(y_stats[0:1], stat_in[corner - 1, 0:1]),
+                        y_stats[1:2] + stat_in[corner - 1, 1:2],
+                    ],
+                    axis=0,
+                )
+                s_copy(beside_y, y_device, s_recv).start()
 
         top, mass = own_stats[0:1], own_stats[1:2]
         for index in range(helpers):

time: 26.6 us -> 26.5 us (level)
  no operation moved by 1% of the time
where the time goes in v7:
time: 26.5 us; the launch traced here: 26.3 us
  Pallas kernels  25.5 us (96%)
  between operations  0.8 us (3%)
    pallas_call x1, Pallas kernels, dense(): pl.pallas_call(dense_kernel, out_shape=(jax.ShapeDtypeStruct((rows, featu...  24.9 us
    pallas_call x1, Pallas kernels, finish(): pl.pallas_call(finish_kernel, out_shape=(jax.ShapeDtypeStruct((rows, feat...  0.7 us

profile of v7, /device:TPU:0, one launch (start us, length us, event | category | flops | bytes accessed | tf_op | source)
XLA Modules:
  0.0 26.3 jit_solution(8069360589060023907)
XLA Ops:
  0.6 24.9 %shard_map.50 = (bf16[128,768]{1,0:T(8,128)(2,1)S(1)}, f32[1,128]{1,0:T(1,128)S(1)}) custom-call(bf16[128,768]{1,0:T(8,128)(2,1)} %emb_hbm.1, s32[1,128]{1,0:T(1,128)} %bitcast.2, s32[1,128]{1,0:T(1,128)} %bitcast.3), custom_call_target="tpu_custom_call" | custom-call | tf_op jit(solution)/shard_map/pallas_call | solution.py:676
  25.5 0.7 %shard_map.51 = (bf16[128,768]{1,0:T(8,128)(2,1)}, bf16[128]{0:T(256)(128)(2,1)}) custom-call(bf16[128,768]{1,0:T(8,128)(2,1)S(1)} %get-tuple-element.4.mean_ref, f32[1,128]{1,0:T(1,128)S(1)} %get-tuple-element.5.best_ref), custom_call_target="tpu_custom_call" | custom-call | tf_op jit(solution)/shard_map/pallas_call | solution.py:651

commit v8 on v7

--- a/solution.py
+++ b/solution.py
@@ -572,7 +572,8 @@
             assist(1)
         else:
             own_stats = own_final()
-        sent(part_out.at[corner - 1, halves[0]], p_send.at[0])
+        if place > 0:
+            sent(part_out.at[corner - 1, halves[0]], p_send.at[0])
         for spot, side in zip(both, (0, 1)):
             p_copy(spot, halves[side]).start()
         if place == 1:
@@ -608,6 +609,8 @@
         sent(keys.at[0:slots, 0], c_send)
         sent(plane.at[0 : corner - 1, 0], q_send.at[1])
         sent(part_out.at[corner - 1, halves[0]], p_send.at[2])
+        if place == 0:
+            sent(part_out.at[corner - 1, halves[0]], p_send.at[0])
         pairs = hops + slots + 3 + 3 + (3 if place > 0 else 0) + len(helps)
         sent(peak.at[0, pl.ds(0, 2 * pairs)], small_send)
         if place > 0:

time: 26.5 us -> 26.5 us (level)
  no operation moved by 1% of the time
where the time goes in v8:
time: 26.5 us; the launch traced here: 26.3 us
  Pallas kernels  25.5 us (96%)
  between operations  0.8 us (3%)
    pallas_call x1, Pallas kernels, dense(): pl.pallas_call(dense_kernel, out_shape=(jax.ShapeDtypeStruct((rows, featu...  24.8 us
    pallas_call x1, Pallas kernels, finish(): pl.pallas_call(finish_kernel, out_shape=(jax.ShapeDtypeStruct((rows, feat...  0.7 us

profile of v8, /device:TPU:0, one launch (start us, length us, event | category | flops | bytes accessed | tf_op | source)
XLA Modules:
  0.0 26.3 jit_solution(4098807050849180031)
XLA Ops:
  0.6 24.8 %shard_map.50 = (bf16[128,768]{1,0:T(8,128)(2,1)S(1)}, f32[1,128]{1,0:T(1,128)S(1)}) custom-call(bf16[128,768]{1,0:T(8,128)(2,1)} %emb_hbm.1, s32[1,128]{1,0:T(1,128)} %bitcast.2, s32[1,128]{1,0:T(1,128)} %bitcast.3), custom_call_target="tpu_custom_call" | custom-call | tf_op jit(solution)/shard_map/pallas_call | solution.py:679
  25.5 0.7 %shard_map.51 = (bf16[128,768]{1,0:T(8,128)(2,1)}, bf16[128]{0:T(256)(128)(2,1)}) custom-call(bf16[128,768]{1,0:T(8,128)(2,1)S(1)} %get-tuple-element.4.mean_ref, f32[1,128]{1,0:T(1,128)S(1)} %get-tuple-element.5.best_ref), custom_call_target="tpu_custom_call" | custom-call | tf_op jit(solution)/shard_map/pallas_call | solution.py:654
